TPU v7x, 256 devices: a whole 4x4x8 slice. The times are simulated.
256 devices in a mesh: grp: 8 (over x_hi, y), blk: 32 (over x_lo, z, core).
Axes of the slice: x: 4 (x_hi: 2, x_lo: 2; x = x_hi * 2 + x_lo), y: 4, z: 8, core: 2. Of those that a mesh axis runs over, the one named last changes fastest.
Arguments:
- queries: bfloat16 [32768, 4096], P(('grp', 'blk')), parts along dimension 0, may hold values from -256 to 256
- new_keys: bfloat16 [32768, 512], P(('grp', 'blk')), parts along dimension 0, may hold values from -6 to 6
- new_values: bfloat16 [32768, 512], P(('grp', 'blk')), parts along dimension 0, may hold values from -6 to 6
- prefix_keys: bfloat16 [32768, 512], P(('grp', 'blk')), parts along dimension 0, may hold values from -6 to 6
- prefix_values: bfloat16 [32768, 512], P(('grp', 'blk')), parts along dimension 0, may hold values from -6 to 6
- block_table: int32 [256, 16], P(('grp', 'blk')), parts along dimension 0, may hold values from 0 to 31, as said below
- prefix_blocks: int32 [256], P(('grp', 'blk')), parts along dimension 0, may hold values from 1 to 16, 320 in all
Outputs:
- attended: bfloat16 [32768, 4096], P(('grp', 'blk')), parts along dimension 0
There are 8 independent parts, one for each index of `grp`. A program takes and returns all parts, laid end to end along the dimension named above; each array names one. Nothing has to cross between parts.
Inputs may be any that keep to these rules, and one draw needn't show every extreme that they name: `block_table`: each row names 16 different prefix blocks; only the first prefix_blocks entries of a row are read. `prefix_blocks`: within each group (each index of grp) the lengths sum to 320.
All inputs are finite; a program needn't handle non-finite values.
Results may differ from a plain program's by a relative error of at most 0.008.
Values may be sent and summed in bfloat16 or wider, within the bound.
No kernel may reach another device: no remote copies, remote signals or barrier semaphores. Data moves between devices by JAX's collectives and lax.ppermute only.
A program may use at most 64 MiB of HBM per device.

v0:
```python
import jax
import jax.numpy as jnp
from jax import lax
from jax.sharding import PartitionSpec as P

KVH = 4
DH = 128
BS = 128
G = 8


def head_major(block, heads):
    rows = block.shape[0]
    return block.reshape(rows, heads, DH).transpose(1, 0, 2)


def absorb(carry, key_block, value_block, usable, query_heads):
    top, total, summed = carry
    scores = jnp.einsum(
        "krd,kld->krl", query_heads, key_block, preferred_element_type=jnp.float32
    ) * DH ** (-0.5)
    scores = jnp.where(usable, scores, -jnp.inf)
    new_top = jnp.maximum(top, jnp.max(scores, axis=-1))
    factor = jnp.exp(top - new_top)
    weights = jnp.exp(scores - new_top[..., None])
    total = factor * total + jnp.sum(weights, axis=-1)
    summed = factor[..., None] * summed + jnp.einsum(
        "krl,kld->krd",
        weights.astype(jnp.bfloat16),
        value_block,
        preferred_element_type=jnp.float32,
    )
    return (new_top, total, summed)


def body(queries, new_keys, new_values, prefix_keys, prefix_values, block_table, prefix_blocks):
    tokens = queries.shape[0]
    query_heads = (
        queries.reshape(tokens, KVH, G, DH).transpose(1, 2, 0, 3).reshape(KVH, G * tokens, DH)
    )
    own_keys = head_major(new_keys, KVH)
    own_values = head_major(new_values, KVH)
    scores = jnp.einsum(
        "krd,kld->krl", query_heads, own_keys, preferred_element_type=jnp.float32
    ) * DH ** (-0.5)
    row_token = jnp.arange(G * tokens, dtype=jnp.int32) % tokens
    causal = jnp.arange(tokens, dtype=jnp.int32)[None, :] <= row_token[:, None]
    scores = jnp.where(causal[None], scores, -jnp.inf)
    top = jnp.max(scores, axis=-1)
    weights = jnp.exp(scores - top[..., None])
    total = jnp.sum(weights, axis=-1)
    summed = jnp.einsum(
        "krl,kld->krd", weights.astype(jnp.bfloat16), own_values, preferred_element_type=jnp.float32
    )
    carry = (top, total, summed)
    table_row = block_table[0]
    length = prefix_blocks[0]
    entries = table_row.shape[0]
    pool_count = lax.axis_size("blk")
    live_entry = jnp.arange(entries, dtype=jnp.int32) < length
    matches = (table_row[None, :] == jnp.arange(pool_count, dtype=jnp.int32)[:, None]) & live_entry[
        None, :
    ]
    used = jnp.any(matches, axis=1)
    state = carry
    piece_keys = lax.all_gather(prefix_keys, "blk", axis=0, tiled=True)
    piece_values = lax.all_gather(prefix_values, "blk", axis=0, tiled=True)
    count = piece_keys.shape[0] // BS
    key_blocks = piece_keys.reshape(count, BS, KVH, DH).transpose(0, 2, 1, 3)
    value_blocks = piece_values.reshape(count, BS, KVH, DH).transpose(0, 2, 1, 3)
    block_ids = jnp.arange(count, dtype=jnp.int32)

    def visit(inner, items):
        key_block, value_block, block_id = items
        return (absorb(inner, key_block, value_block, used[block_id], query_heads), None)

    state, _ = lax.scan(visit, state, (key_blocks, value_blocks, block_ids))
    carry = state
    top, total, summed = carry
    result = summed / total[..., None]
    result = result.reshape(KVH, G, tokens, DH).transpose(2, 0, 1, 3).reshape(tokens, KVH * G * DH)
    return result.astype(jnp.bfloat16)


def solution(mesh):
    in_specs = (
        P(("grp", "blk"), None),
        P(("grp", "blk"), None),
        P(("grp", "blk"), None),
        P(("grp", "blk"), None),
        P(("grp", "blk"), None),
        P(("grp", "blk"), None),
        P(("grp", "blk")),
    )
    out_specs = P(("grp", "blk"), None)
    return jax.shard_map(body, mesh=mesh, in_specs=in_specs, out_specs=out_specs, check_vma=False)
```

profile of v0, /device:TPU:1, one launch (start us, length us, event | category | flops | bytes accessed | tf_op | source)
XLA Modules:
  0.0 444.6 jit_solution(10240727030767275506)
XLA Ops:
  12.5 67.8 %all-gather.5.cloned.1.call-done = bf16[4096,512]{1,0:T(8,128)(2,1)} async-done(((bf16[128,512]{1,0:T(8,128)(2,1)}), bf16[4096,512]{1,0:T(8,128)(2,1)}) %all-gather.5.cloned.1.call-update) | async-done | bytes 4194320 | tf_op jit(solution)/shard_map/all_gather | solution.py:67
  80.3 6.9 %reshape.65 = bf16[32,128,4,128]{3,2,1,0:T(4,128)(2,1)} reshape(bf16[4096,512]{1,0:T(8,128)(2,1)} %all-gather.5.cloned.1.call-done) | data formatting | bytes 8388608 | tf_op jit(solution)/shard_map/reshape | solution.py:70
  87.2 5.3 %copy.57 = bf16[32,128,4,128]{3,1,2,0:T(8,128)(2,1)} copy(bf16[32,128,4,128]{3,2,1,0:T(4,128)(2,1)} %reshape.65) | data formatting | bytes 8388608 | tf_op jit(solution)/shard_map/transpose | solution.py:70
  92.5 56.1 %all-gather.3.cloned.1.call-done = bf16[4096,512]{1,0:T(8,128)(2,1)} async-done(((bf16[128,512]{1,0:T(8,128)(2,1)}), bf16[4096,512]{1,0:T(8,128)(2,1)}) %all-gather.3.cloned.1.call-update) | async-done | bytes 4194320 | tf_op jit(solution)/shard_map/all_gather | solution.py:66
  148.6 6.9 %reshape.64 = bf16[32,128,4,128]{3,2,1,0:T(4,128)(2,1)} reshape(bf16[4096,512]{1,0:T(8,128)(2,1)} %all-gather.3.cloned.1.call-done) | data formatting | bytes 8388608 | tf_op jit(solution)/shard_map/reshape | solution.py:69
  155.6 5.3 %copy.58 = bf16[32,128,4,128]{3,1,2,0:T(8,128)(2,1)} copy(bf16[32,128,4,128]{3,2,1,0:T(4,128)(2,1)} %reshape.64) | data formatting | bytes 8388608 | tf_op jit(solution)/shard_map/transpose | solution.py:69
  160.9 274.0 %while.14 = (s32[]{:T(128)}, f32[4,1024]{1,0:T(4,128)S(1)}, f32[4,1024]{1,0:T(4,128)S(1)}, f32[4,1024,128]{2,1,0:T(8,128)S(1)}, s32[32]{0:T(128)S(1)}, /*index=5...) while((s32[]{:T(128)}, f32[4,1024]{1,0:T(4,128)S(1)}, ...), condition=%wide.region_6.7_spmd, body=%wide.region_3.6_spmd.sunk | while | flops 275259392 | bytes 12060842 | solution.py:77
  166.7 2.7 multiply_add_fusion.5
  175.3 2.7 multiply_add_fusion.5
  183.9 2.7 multiply_add_fusion.5
  192.4 2.7 multiply_add_fusion.5
  209.6 2.7 multiply_add_fusion.5
  218.1 2.7 multiply_add_fusion.5
  226.7 2.7 multiply_add_fusion.5
  235.3 2.7 multiply_add_fusion.5
  243.8 2.7 multiply_add_fusion.5
  252.4 2.7 multiply_add_fusion.5
  260.9 2.7 multiply_add_fusion.5
  269.5 2.7 multiply_add_fusion.5
  278.1 2.7 multiply_add_fusion.5
  286.6 2.7 multiply_add_fusion.5
  295.2 2.7 multiply_add_fusion.5
  303.8 2.7 multiply_add_fusion.5
  312.3 2.7 multiply_add_fusion.5
  320.9 2.7 multiply_add_fusion.5
  329.5 2.7 multiply_add_fusion.5
  338.0 2.7 multiply_add_fusion.5
  346.6 2.7 multiply_add_fusion.5
  355.2 2.7 multiply_add_fusion.5
  372.3 2.7 multiply_add_fusion.5
  380.8 2.7 multiply_add_fusion.5
  389.4 2.7 multiply_add_fusion.5
  (254 shorter events, 158.1 us)
Async XLA Ops:
  6.5 4.2 copy-start
  6.5 73.8 %all-gather.5.cloned.1.call-start = ((), (), s32[]{:S(2)}) async-start(), calls=%async_computation.1 | async-start | bytes 4325376 | tf_op jit(solution)/shard_map/all_gather | solution.py:67
  7.3 141.4 %all-gather.3.cloned.1.call-start = ((), (), s32[]{:S(2)}) async-start(), calls=%async_computation | async-start | bytes 4325376 | tf_op jit(solution)/shard_map/all_gather | solution.py:66
  8.0 2.6 copy-start.2
  10.8 1.0 copy-start.1
Sparse Core Ops, SparseCore 0:
  9.2 71.0 all-gather.4
  82.2 66.4 all-gather.2
where the time goes:
time: 449 us; the launch traced here: 445 us
  matrix products  149 us (33%)
  waiting for transfers between devices  125 us (28%)
  local copies, waits for them, and re-layouts  64.4 us (14%)
  loops' own time  56.5 us (13%)
  other arithmetic  34.9 us (8%)
  between operations  14.2 us (3%)
    dot_general x32, matrix products, absorb(): jnp.einsum('krl,kld->krd', weights.astype(jnp.bfloat16), value_block, pre...  86.5 us
    all_gather x1, waiting for transfers between devices, body(): piece_values = lax.all_gather(prefix_values, 'blk', axis=0, tiled=True)  67.8 us
    dot_general x32, matrix products, absorb(): jnp.einsum('krd,kld->krl', query_heads, key_block, preferred_element_type...  61.6 us
    another operation x1, loops' own time, body(): state, _ = lax.scan(visit, state, (key_blocks, value_blocks, block_ids))  56.5 us
    all_gather x1, waiting for transfers between devices, body(): piece_keys = lax.all_gather(prefix_keys, 'blk', axis=0, tiled=True)  56.1 us
    reduce_sum x32, other arithmetic, absorb(): total = factor * total + jnp.sum(weights, axis=-1)  32.6 us
    dynamic_slice x32, local copies, waits for them, and re-layouts, visit(): used[block_id]  18 us
    dynamic_slice x32, local copies, waits for them, and re-layouts, body(): state, _ = lax.scan(visit, state, (key_blocks, value_blocks, block_ids))  17.9 us
  transfers between devices with their start and end apart: 2, of which 2 were waited for; matrix products, arithmetic and copies ran while one was open for 4% of the time, Pallas kernels for 0%

commit v1 on v0

v1 whole, which is shorter than its diff:
```python
import functools
import math

import jax
import jax.numpy as jnp
from jax import lax
from jax.experimental import pallas as pl
from jax.experimental.pallas import tpu as pltpu
from jax.sharding import PartitionSpec as P

H = 32
KVH = 4
DH = 128
BS = 128
G = 8
KW = KVH * DH
CHUNK = 4
MAXB = 16
CAP = MAXB + CHUNK
ROWS = 256
HEADS = ROWS // BS
SCALE = DH**-0.5 * math.log2(math.e)


def index(x, z, c):
    return ((x % 2) * 8 + z % 8) * 2 + c % 2


def pairs(target):
    return [
        (index(x, z, c), index(*target(x, z, c)))
        for x in range(2)
        for z in range(8)
        for c in range(2)
    ]


AHEAD = pairs(lambda x, z, c: (x, z + 1 - 2 * c, c))
BACK = pairs(lambda x, z, c: (x, z - 1 + 2 * c, c))
ACROSS = pairs(lambda x, z, c: (x + 1, z, c))
SIBLING = pairs(lambda x, z, c: (x, z, c + 1))


def send(piece, table):
    return lax.ppermute(piece, "blk", table)


def gather(piece):
    x0 = send(piece, ACROSS)
    a1, b1 = send(piece, AHEAD), send(piece, BACK)
    a2, b2 = send(a1, AHEAD), send(b1, BACK)
    xa1, xb1 = send(x0, AHEAD), send(x0, BACK)
    xa2, xb2 = send(a2, ACROSS), send(b2, ACROSS)
    a3, b3 = send(a2, AHEAD), send(b2, BACK)
    xb3, xa3 = send(xb2, BACK), send(a3, ACROSS)
    a4 = send(a3, AHEAD)
    xa4 = send(a4, ACROSS)
    held = [
        (piece, 0, 0), (x0, 1, 0),
        (a1, 0, -1), (b1, 0, 1), (xa1, 1, -1), (xb1, 1, 1),
        (a2, 0, -2), (b2, 0, 2), (xa2, 1, -2), (xb2, 1, 2),
        (a3, 0, -3), (b3, 0, 3), (xa3, 1, -3), (xb3, 1, 3),
        (a4, 0, -4), (xa4, 1, -4),
    ]
    me = lax.axis_index("blk")
    x, z, c = me // 16, (me // 2) % 8, me % 2
    way = 1 - 2 * c
    pieces, owners = [], []
    for array, dx, dz in held:
        pieces.append(array)
        owners.append((((x + dx) % 2) * 8 + (z + dz * way) % 8) * 2 + c)
        pieces.append(send(array, SIBLING))
        owners.append((((x + dx) % 2) * 8 + (z - dz * way) % 8) * 2 + 1 - c)
    return pieces, jnp.stack(owners)


def attend(slots, used_ref, place_ref, count_ref, q_ref, nk_ref, nv_ref, *rest):
    pieces = rest[:slots]
    out_ref, kv_ref, acc_ref, top_ref, sems = rest[slots:]
    count = count_ref[0]

    for i in range(slots):
        @pl.when(used_ref[i] > 0)
        def _(i=i):
            pltpu.make_async_copy(pieces[i], kv_ref.at[place_ref[i]], sems.at[i]).start()

    ones = jnp.ones((BS, DH), jnp.bfloat16)
    many = jnp.ones((CHUNK * BS, DH), jnp.bfloat16)
    row = lax.broadcasted_iota(jnp.int32, (ROWS, BS), 0) % BS
    causal = lax.broadcasted_iota(jnp.int32, (ROWS, BS), 1) <= row
    lane = lax.broadcasted_iota(jnp.int32, (ROWS, CHUNK * BS), 1)
    groups = G // HEADS

    def query(t):
        first = t * HEADS
        return jnp.concatenate(
            [q_ref[:, pl.ds(pl.multiple_of((first + j) * DH, DH), DH)] for j in range(HEADS)], axis=0
        )

    def dot_t(a, b):
        return lax.dot_general(a, b, (((1,), (1,)), ((), ())), preferred_element_type=jnp.float32)

    @pl.loop(0, H // HEADS)
    def _(t):
        g = t // groups
        col = pl.ds(pl.multiple_of(g * DH, DH), DH)
        s = jnp.where(causal, dot_t(query(t), nk_ref[:, col]) * SCALE, -jnp.inf)
        top = jnp.max(s, axis=1, keepdims=True)
        w = jnp.exp2(s - top).astype(jnp.bfloat16)
        rhs = jnp.concatenate([nv_ref[:, col], ones], axis=1)
        rows = pl.ds(pl.multiple_of(t * ROWS, ROWS), ROWS)
        acc_ref[rows, :] = jnp.dot(w, rhs, preferred_element_type=jnp.float32)
        top_ref[rows, :] = jnp.broadcast_to(top, (ROWS, DH))

    for i in range(slots):
        @pl.when(used_ref[i] > 0)
        def _(i=i):
            pltpu.make_async_copy(pieces[i], kv_ref.at[place_ref[i]], sems.at[i]).wait()

    for j in range(CHUNK - 1):
        kv_ref[count + j, :, KW:] = jnp.zeros((BS, KW), jnp.bfloat16)

    @pl.loop(0, (count + CHUNK - 1) // CHUNK)
    def _(k):
        live = (count - k * CHUNK) * BS
        blocks = pl.ds(k * CHUNK, CHUNK)

        @pl.loop(0, H // HEADS)
        def _(t):
            g = t // groups
            rows = pl.ds(pl.multiple_of(t * ROWS, ROWS), ROWS)
            key = kv_ref[blocks, :, pl.ds(pl.multiple_of(g * DH, DH), DH)].reshape(CHUNK * BS, DH)
            value = kv_ref[blocks, :, pl.ds(pl.multiple_of(KW + g * DH, DH), DH)].reshape(CHUNK * BS, DH)
            s = jnp.where(lane < live, dot_t(query(t), key) * SCALE, -jnp.inf)
            old = top_ref[rows, :]
            top = jnp.maximum(old, jnp.max(s, axis=1, keepdims=True))
            factor = jnp.exp2(old - top)
            w = jnp.exp2(s - jnp.tile(top, (1, CHUNK))).astype(jnp.bfloat16)
            rhs = jnp.concatenate([value, many], axis=1)
            acc_ref[rows, :] = acc_ref[rows, :] * jnp.tile(factor, (1, 2)) + jnp.dot(
                w, rhs, preferred_element_type=jnp.float32
            )
            top_ref[rows, :] = top

    @pl.loop(0, H // HEADS)
    def _(t):
        for j in range(HEADS):
            rows = pl.ds(pl.multiple_of(t * ROWS + j * BS, BS), BS)
            total = acc_ref[rows, DH:]
            out_ref[:, pl.ds(pl.multiple_of((t * HEADS + j) * DH, DH), DH)] = (
                acc_ref[rows, :DH] / total
            ).astype(jnp.bfloat16)


def body(queries, new_keys, new_values, prefix_keys, prefix_values, block_table, prefix_blocks):
    piece = jnp.concatenate([prefix_keys, prefix_values], axis=1)
    pieces, owners = gather(piece)
    slots = len(pieces)
    live = jnp.arange(MAXB, dtype=jnp.int32) < prefix_blocks[0]
    used = jnp.any((block_table[0][None, :] == owners[:, None]) & live[None, :], axis=1).astype(jnp.int32)
    order = jnp.arange(slots, dtype=jnp.int32)
    place = jnp.sum(jnp.where(order[None, :] < order[:, None], used[None, :], 0), axis=1)
    count = jnp.sum(used)[None]
    vmem = pl.BlockSpec(memory_space=pltpu.VMEM)
    smem = pl.BlockSpec(memory_space=pltpu.SMEM)
    return pl.pallas_call(
        functools.partial(attend, slots),
        out_shape=jax.ShapeDtypeStruct(queries.shape, jnp.bfloat16),
        in_specs=[smem] * 3 + [vmem] * 3 + [pl.BlockSpec(memory_space=pl.ANY)] * slots,
        out_specs=vmem,
        scratch_shapes=[
            pltpu.VMEM((CAP, BS, 2 * KW), jnp.bfloat16),
            pltpu.VMEM((H * BS, 2 * DH), jnp.float32),
            pltpu.VMEM((H * BS, DH), jnp.float32),
            pltpu.SemaphoreType.DMA((slots,)),
        ],
        compiler_params=pltpu.CompilerParams(vmem_limit_bytes=40 << 20),
    )(used, place, count, queries, new_keys, new_values, *pieces)


def solution(mesh):
    spec = P(("grp", "blk"), None)
    return jax.shard_map(
        body, mesh=mesh, in_specs=(spec,) * 6 + (P(("grp", "blk")),), out_specs=spec, check_vma=False
    )
```

time: 449 us -> 122 us (0.27)
  the two profiles are of different devices: /device:TPU:1 before, /device:TPU:19 now
where the time goes in v1:
time: 122 us; the launch traced here: 121 us
  Pallas kernels  46.4 us (38%)
  starting transfers between devices  40.8 us (33%)
  local copies, waits for them, and re-layouts  17.9 us (15%)
  waiting for transfers between devices  14.2 us (12%)
    pallas_call x1, Pallas kernels, body(): pl.pallas_call(functools.partial(attend, slots), out_shape=jax.ShapeDtype...  46.4 us
    ppermute x31, starting transfers between devices, send(): return lax.ppermute(piece, 'blk', table)  40.8 us
    unnamed x51, local copies, waits for them, and re-layouts  17.8 us
    ppermute x31, waiting for transfers between devices, send(): return lax.ppermute(piece, 'blk', table)  14.2 us
  transfers between devices with their start and end apart: 31, of which 9 were waited for; matrix products, arithmetic and copies ran while one was open for 1% of the time, Pallas kernels for 0%

profile of v1, /device:TPU:19, one launch (start us, length us, event | category | flops | bytes accessed | tf_op | source)
XLA Modules:
  0.0 121.2 jit_solution(13999744048978797271)
XLA Ops:
  0.0 1.0 constant_dynamic-update-slice_fusion.1
  1.0 1.7 %collective-permute-start.5 = (bf16[128,1024]{1,0:T(8,128)(2,1)S(1)}, bf16[128,1024]{1,0:T(8,128)(2,1)S(1)}, u32[]{:S(2)}, u32[]{:S(2)}) collective-permute-start(bf16[128,1024]{1,0:T(8,128)(2,1)S(1)} %constant_dynamic-update-slice_fusion.rest_0_), channel_id=1, source_target_pairs={{0,14},{1,3},{2,0},{3,5},{4,2},{5,7},{6,4},{7,9},{8,6},{9,11},{10,... | collective-permute-start | bytes 786440 | tf_op jit(solution)/shard_map/ppermute | solution.py:45
  2.8 4.0 %collective-permute-start.3 = (bf16[128,1024]{1,0:T(8,128)(2,1)S(1)}, bf16[128,1024]{1,0:T(8,128)(2,1)S(1)}, u32[]{:S(2)}, u32[]{:S(2)}) collective-permute-start(bf16[128,1024]{1,0:T(8,128)(2,1)S(1)} %constant_dynamic-update-slice_fusion.rest_0_), channel_id=1, source_target_pairs={{0,2},{1,15},{2,4},{3,1},{4,6},{5,3},{6,8},{7,5},{8,10},{9,7},{10,... | collective-permute-start | bytes 786440 | tf_op jit(solution)/shard_map/ppermute | solution.py:45
  7.0 1.1 collective-permute-start
  8.2 2.3 %collective-permute-done.5.rest_6_ = bf16[128,1024]{1,0:T(8,128)(2,1)S(1)} collective-permute-done((bf16[128,1024]{1,0:T(8,128)(2,1)S(1)}, bf16[128,1024]{1,0:T(8,128)(2,1)S(1)}, u32[]{:S(2)}, u32[]{:S(2)}) %collective-permute-start.5) | collective-permute-done | bytes 262176 | tf_op jit(solution)/shard_map/ppermute | solution.py:45
  10.5 6.5 %collective-permute-start.6 = (bf16[128,1024]{1,0:T(8,128)(2,1)S(1)}, bf16[128,1024]{1,0:T(8,128)(2,1)S(1)}, u32[]{:S(2)}, u32[]{:S(2)}) collective-permute-start(bf16[128,1024]{1,0:T(8,128)(2,1)S(1)} %collective-permute-done.5.rest_6_), channel_id=1, source_target_pairs={{0,1},{1,0},{2,3},{3,2},{4,5},{5,4},{6,7},{7,6},{8,9},{9,8},{10,11... | collective-permute-start | bytes 786440 | tf_op jit(solution)/shard_map/ppermute | solution.py:45
  17.2 1.4 %collective-permute-start.9 = (bf16[128,1024]{1,0:T(8,128)(2,1)S(1)}, bf16[128,1024]{1,0:T(8,128)(2,1)S(1)}, u32[]{:S(2)}, u32[]{:S(2)}) collective-permute-start(bf16[128,1024]{1,0:T(8,128)(2,1)S(1)} %collective-permute-done.1.rest_2_), channel_id=1, source_target_pairs={{0,14},{1,3},{2,0},{3,5},{4,2},{5,7},{6,4},{7,9},{8,6},{9,11},{10,... | collective-permute-start | bytes 786440 | tf_op jit(solution)/shard_map/ppermute | solution.py:45
  18.6 1.5 %collective-permute-start.7 = (bf16[128,1024]{1,0:T(8,128)(2,1)S(1)}, bf16[128,1024]{1,0:T(8,128)(2,1)S(1)}, u32[]{:S(2)}, u32[]{:S(2)}) collective-permute-start(bf16[128,1024]{1,0:T(8,128)(2,1)S(1)} %collective-permute-done.1.rest_2_), channel_id=1, source_target_pairs={{0,2},{1,15},{2,4},{3,1},{4,6},{5,3},{6,8},{7,5},{8,10},{9,7},{10,... | collective-permute-start | bytes 786440 | tf_op jit(solution)/shard_map/ppermute | solution.py:45
  20.1 3.6 %collective-permute-start.2 = (bf16[128,1024]{1,0:T(8,128)(2,1)S(1)}, bf16[128,1024]{1,0:T(8,128)(2,1)S(1)}, u32[]{:S(2)}, u32[]{:S(2)}) collective-permute-start(bf16[128,1024]{1,0:T(8,128)(2,1)S(1)} %collective-permute-done.1.rest_2_), channel_id=1, source_target_pairs={{0,1},{1,0},{2,3},{3,2},{4,5},{5,4},{6,7},{7,6},{8,9},{9,8},{10,11... | collective-permute-start | bytes 786440 | tf_op jit(solution)/shard_map/ppermute | solution.py:45
  24.4 2.2 %collective-permute-done.9.rest_10_ = bf16[128,1024]{1,0:T(8,128)(2,1)S(1)} collective-permute-done((bf16[128,1024]{1,0:T(8,128)(2,1)S(1)}, bf16[128,1024]{1,0:T(8,128)(2,1)S(1)}, u32[]{:S(2)}, u32[]{:S(2)}) %collective-permute-start.9) | collective-permute-done | bytes 262176 | tf_op jit(solution)/shard_map/ppermute | solution.py:45
  26.7 2.6 %collective-permute-start.14 = (bf16[128,1024]{1,0:T(8,128)(2,1)S(1)}, bf16[128,1024]{1,0:T(8,128)(2,1)S(1)}, u32[]{:S(2)}, u32[]{:S(2)}) collective-permute-start(bf16[128,1024]{1,0:T(8,128)(2,1)S(1)} %collective-permute-done.13.rest_14_), channel_id=1, source_target_pairs={{0,1},{1,0},{2,3},{3,2},{4,5},{5,4},{6,7},{7,6},{8,9},{9,8},{10,11... | collective-permute-start | bytes 786440 | tf_op jit(solution)/shard_map/ppermute | solution.py:45
  29.3 3.4 %collective-permute-start.19 = (bf16[128,1024]{1,0:T(8,128)(2,1)S(1)}, bf16[128,1024]{1,0:T(8,128)(2,1)}, u32[]{:S(2)}, u32[]{:S(2)}) collective-permute-start(bf16[128,1024]{1,0:T(8,128)(2,1)S(1)} %collective-permute-done.11.rest_12_), channel_id=1, source_target_pairs={{0,2},{1,15},{2,4},{3,1},{4,6},{5,3},{6,8},{7,5},{8,10},{9,7},{10,... | collective-permute-start | bytes 786440 | tf_op jit(solution)/shard_map/ppermute | solution.py:45
  33.8 1.8 %collective-permute-start.12 = (bf16[128,1024]{1,0:T(8,128)(2,1)S(1)}, bf16[128,1024]{1,0:T(8,128)(2,1)S(1)}, u32[]{:S(2)}, u32[]{:S(2)}) collective-permute-start(bf16[128,1024]{1,0:T(8,128)(2,1)S(1)} %collective-permute-done.11.rest_12_), channel_id=1, source_target_pairs={{0,1},{1,0},{2,3},{3,2},{4,5},{5,4},{6,7},{7,6},{8,9},{9,8},{10,11... | collective-permute-start | bytes 786440 | tf_op jit(solution)/shard_map/ppermute | solution.py:45
  38.3 3.8 %collective-permute-start.22 = (bf16[128,1024]{1,0:T(8,128)(2,1)S(1)}, bf16[128,1024]{1,0:T(8,128)(2,1)S(1)}, u32[]{:S(2)}, u32[]{:S(2)}) collective-permute-start(bf16[128,1024]{1,0:T(8,128)(2,1)S(1)} %collective-permute-done.21.rest_22_), channel_id=1, source_target_pairs={{0,1},{1,0},{2,3},{3,2},{4,5},{5,4},{6,7},{7,6},{8,9},{9,8},{10,11... | collective-permute-start | bytes 786440 | tf_op jit(solution)/shard_map/ppermute | solution.py:45
  44.0 0.9 collective-permute-start.25
  45.6 1.8 %collective-permute-start.18 = (bf16[128,1024]{1,0:T(8,128)(2,1)}, bf16[128,1024]{1,0:T(8,128)(2,1)}, u32[]{:S(2)}, u32[]{:S(2)}) collective-permute-start(bf16[128,1024]{1,0:T(8,128)(2,1)} %collective-permute-done.17.rest_18_), channel_id=1, source_target_pairs={{0,1},{1,0},{2,3},{3,2},{4,5},{5,4},{6,7},{7,6},{8,9},{9,8},{10,11... | collective-permute-start | bytes 786440 | tf_op jit(solution)/shard_map/ppermute | solution.py:45
  51.4 1.3 %collective-permute-done.25.rest_26_ = bf16[128,1024]{1,0:T(8,128)(2,1)} collective-permute-done((bf16[128,1024]{1,0:T(8,128)(2,1)}, bf16[128,1024]{1,0:T(8,128)(2,1)}, u32[]{:S(2)}, u32[]{:S(2)}) %collective-permute-start.25) | collective-permute-done | bytes 262176 | tf_op jit(solution)/shard_map/ppermute | solution.py:45
  52.8 1.4 %collective-permute-start.16 = (bf16[128,1024]{1,0:T(8,128)(2,1)}, bf16[128,1024]{1,0:T(8,128)(2,1)S(1)}, u32[]{:S(2)}, u32[]{:S(2)}) collective-permute-start(bf16[128,1024]{1,0:T(8,128)(2,1)} %copy-done.11), channel_id=1, source_target_pairs={{0,1},{1,0},{2,3},{3,2},{4,5},{5,4},{6,7},{7,6},{8,9},{9,8},{10,11... | collective-permute-start | bytes 786440 | tf_op jit(solution)/shard_map/ppermute | solution.py:45
  54.3 2.1 %collective-permute-done.23.rest_24_ = bf16[128,1024]{1,0:T(8,128)(2,1)} collective-permute-done((bf16[128,1024]{1,0:T(8,128)(2,1)}, bf16[128,1024]{1,0:T(8,128)(2,1)}, u32[]{:S(2)}, u32[]{:S(2)}) %collective-permute-start.23) | collective-permute-done | bytes 262176 | tf_op jit(solution)/shard_map/ppermute | solution.py:45
  56.4 1.2 collective-permute-start.26
  57.6 4.4 %collective-permute-done.29.rest_30_ = bf16[128,1024]{1,0:T(8,128)(2,1)} collective-permute-done((bf16[128,1024]{1,0:T(8,128)(2,1)}, bf16[128,1024]{1,0:T(8,128)(2,1)}, u32[]{:S(2)}, u32[]{:S(2)}) %collective-permute-start.29) | collective-permute-done | bytes 262176 | tf_op jit(solution)/shard_map/ppermute | solution.py:45
  64.2 0.9 copy-done.2
  65.1 0.9 copy-done.4
  66.1 0.9 copy-done.6
  67.0 0.9 copy-done.8
  68.0 0.9 copy-done.10
  68.9 0.9 copy-done.12
  69.9 0.9 copy-done.14
  70.8 0.9 copy-done.16
  71.8 0.9 copy-done.18
  72.7 0.9 copy-done.20
  74.6 46.4 %shard_map.73 = bf16[128,4096]{1,0:T(8,128)(2,1)} custom-call(s32[32]{0:T(128)S(1)} %convert_element_type.3.used_ref, s32[32]{0:T(128)S(1)} %select_reduce_fusion.place_ref, s32[1]{0:T(128)} %bitcast.34.count_ref, bf16[128,4096]{1,0:T(8,128)(2,1)S(1)} %copy-done, bf16[128,512]{1,0:T(8,128)(2,1)S(1)} %copy-done.21, bf16[128,512]{1,0:T(8,128)(2,1)S(1)} %copy-done.22, ...), custom_call_target="tpu_custom_call" | custom-call | tf_op jit(solution)/shard_map/pallas_call | solution.py:166
  (89 shorter events, 14.0 us)
Async XLA Ops:
  0.0 64.2 %copy-start = (bf16[128,4096]{1,0:T(8,128)(2,1)S(1)}, bf16[128,4096]{1,0:T(8,128)(2,1)}, u32[]{:S(2)}) copy-start(bf16[128,4096]{1,0:T(8,128)(2,1)} %q_ref.1) | copy-start | bytes 3145732
  1.0 9.4 %collective-permute-start.5 = (bf16[128,1024]{1,0:T(8,128)(2,1)S(1)}, bf16[128,1024]{1,0:T(8,128)(2,1)S(1)}, u32[]{:S(2)}, u32[]{:S(2)}) collective-permute-start(bf16[128,1024]{1,0:T(8,128)(2,1)S(1)} %constant_dynamic-update-slice_fusion.rest_0_), channel_id=1, source_target_pairs={{0,14},{1,3},{2,0},{3,5},{4,2},{5,7},{6,4},{7,9},{8,6},{9,11},{10,... | collective-permute-start | bytes 786440 | tf_op jit(solution)/shard_map/ppermute | solution.py:45
  2.8 14.2 %collective-permute-start.3 = (bf16[128,1024]{1,0:T(8,128)(2,1)S(1)}, bf16[128,1024]{1,0:T(8,128)(2,1)S(1)}, u32[]{:S(2)}, u32[]{:S(2)}) collective-permute-start(bf16[128,1024]{1,0:T(8,128)(2,1)S(1)} %constant_dynamic-update-slice_fusion.rest_0_), channel_id=1, source_target_pairs={{0,2},{1,15},{2,4},{3,1},{4,6},{5,3},{6,8},{7,5},{8,10},{9,7},{10,... | collective-permute-start | bytes 786440 | tf_op jit(solution)/shard_map/ppermute | solution.py:45
  6.8 10.4 %collective-permute-start.1 = (bf16[128,1024]{1,0:T(8,128)(2,1)S(1)}, bf16[128,1024]{1,0:T(8,128)(2,1)S(1)}, u32[]{:S(2)}, u32[]{:S(2)}) collective-permute-start(bf16[128,1024]{1,0:T(8,128)(2,1)S(1)} %constant_dynamic-update-slice_fusion.rest_0_), channel_id=1, source_target_pairs={{0,16},{1,17},{2,18},{3,19},{4,20},{5,21},{6,22},{7,23},{8,24},{9,... | collective-permute-start | bytes 786440 | tf_op jit(solution)/shard_map/ppermute | solution.py:45
  7.0 10.1 %collective-permute-start = (bf16[128,1024]{1,0:T(8,128)(2,1)S(1)}, bf16[128,1024]{1,0:T(8,128)(2,1)S(1)}, u32[]{:S(2)}, u32[]{:S(2)}) collective-permute-start(bf16[128,1024]{1,0:T(8,128)(2,1)S(1)} %constant_dynamic-update-slice_fusion.rest_0_), channel_id=1, source_target_pairs={{0,1},{1,0},{2,3},{3,2},{4,5},{5,4},{6,7},{7,6},{8,9},{9,8},{10,11... | collective-permute-start | bytes 786440 | tf_op jit(solution)/shard_map/ppermute | solution.py:45
  10.5 8.1 %collective-permute-start.13 = (bf16[128,1024]{1,0:T(8,128)(2,1)S(1)}, bf16[128,1024]{1,0:T(8,128)(2,1)S(1)}, u32[]{:S(2)}, u32[]{:S(2)}) collective-permute-start(bf16[128,1024]{1,0:T(8,128)(2,1)S(1)} %collective-permute-done.5.rest_6_), channel_id=1, source_target_pairs={{0,14},{1,3},{2,0},{3,5},{4,2},{5,7},{6,4},{7,9},{8,6},{9,11},{10,... | collective-permute-start | bytes 786440 | tf_op jit(solution)/shard_map/ppermute | solution.py:45
  10.5 9.6 %collective-permute-start.6 = (bf16[128,1024]{1,0:T(8,128)(2,1)S(1)}, bf16[128,1024]{1,0:T(8,128)(2,1)S(1)}, u32[]{:S(2)}, u32[]{:S(2)}) collective-permute-start(bf16[128,1024]{1,0:T(8,128)(2,1)S(1)} %collective-permute-done.5.rest_6_), channel_id=1, source_target_pairs={{0,1},{1,0},{2,3},{3,2},{4,5},{5,4},{6,7},{7,6},{8,9},{9,8},{10,11... | collective-permute-start | bytes 786440 | tf_op jit(solution)/shard_map/ppermute | solution.py:45
  17.0 7.2 %collective-permute-start.11 = (bf16[128,1024]{1,0:T(8,128)(2,1)S(1)}, bf16[128,1024]{1,0:T(8,128)(2,1)S(1)}, u32[]{:S(2)}, u32[]{:S(2)}) collective-permute-start(bf16[128,1024]{1,0:T(8,128)(2,1)S(1)} %collective-permute-done.3.rest_4_), channel_id=1, source_target_pairs={{0,2},{1,15},{2,4},{3,1},{4,6},{5,3},{6,8},{7,5},{8,10},{9,7},{10,... | collective-permute-start | bytes 786440 | tf_op jit(solution)/shard_map/ppermute | solution.py:45
  17.2 7.0 %collective-permute-start.4 = (bf16[128,1024]{1,0:T(8,128)(2,1)S(1)}, bf16[128,1024]{1,0:T(8,128)(2,1)S(1)}, u32[]{:S(2)}, u32[]{:S(2)}) collective-permute-start(bf16[128,1024]{1,0:T(8,128)(2,1)S(1)} %collective-permute-done.3.rest_4_), channel_id=1, source_target_pairs={{0,1},{1,0},{2,3},{3,2},{4,5},{5,4},{6,7},{7,6},{8,9},{9,8},{10,11... | collective-permute-start | bytes 786440 | tf_op jit(solution)/shard_map/ppermute | solution.py:45
  17.2 9.5 %collective-permute-start.9 = (bf16[128,1024]{1,0:T(8,128)(2,1)S(1)}, bf16[128,1024]{1,0:T(8,128)(2,1)S(1)}, u32[]{:S(2)}, u32[]{:S(2)}) collective-permute-start(bf16[128,1024]{1,0:T(8,128)(2,1)S(1)} %collective-permute-done.1.rest_2_), channel_id=1, source_target_pairs={{0,14},{1,3},{2,0},{3,5},{4,2},{5,7},{6,4},{7,9},{8,6},{9,11},{10,... | collective-permute-start | bytes 786440 | tf_op jit(solution)/shard_map/ppermute | solution.py:45
  18.6 10.8 %collective-permute-start.7 = (bf16[128,1024]{1,0:T(8,128)(2,1)S(1)}, bf16[128,1024]{1,0:T(8,128)(2,1)S(1)}, u32[]{:S(2)}, u32[]{:S(2)}) collective-permute-start(bf16[128,1024]{1,0:T(8,128)(2,1)S(1)} %collective-permute-done.1.rest_2_), channel_id=1, source_target_pairs={{0,2},{1,15},{2,4},{3,1},{4,6},{5,3},{6,8},{7,5},{8,10},{9,7},{10,... | collective-permute-start | bytes 786440 | tf_op jit(solution)/shard_map/ppermute | solution.py:45
  20.1 12.7 %collective-permute-start.2 = (bf16[128,1024]{1,0:T(8,128)(2,1)S(1)}, bf16[128,1024]{1,0:T(8,128)(2,1)S(1)}, u32[]{:S(2)}, u32[]{:S(2)}) collective-permute-start(bf16[128,1024]{1,0:T(8,128)(2,1)S(1)} %collective-permute-done.1.rest_2_), channel_id=1, source_target_pairs={{0,1},{1,0},{2,3},{3,2},{4,5},{5,4},{6,7},{7,6},{8,9},{9,8},{10,11... | collective-permute-start | bytes 786440 | tf_op jit(solution)/shard_map/ppermute | solution.py:45
  24.2 9.6 %collective-permute-start.21 = (bf16[128,1024]{1,0:T(8,128)(2,1)S(1)}, bf16[128,1024]{1,0:T(8,128)(2,1)S(1)}, u32[]{:S(2)}, u32[]{:S(2)}) collective-permute-start(bf16[128,1024]{1,0:T(8,128)(2,1)S(1)} %collective-permute-done.13.rest_14_), channel_id=1, source_target_pairs={{0,14},{1,3},{2,0},{3,5},{4,2},{5,7},{6,4},{7,9},{8,6},{9,11},{10,... | collective-permute-start | bytes 786440 | tf_op jit(solution)/shard_map/ppermute | solution.py:45
  24.2 11.5 %collective-permute-start.17 = (bf16[128,1024]{1,0:T(8,128)(2,1)S(1)}, bf16[128,1024]{1,0:T(8,128)(2,1)}, u32[]{:S(2)}, u32[]{:S(2)}) collective-permute-start(bf16[128,1024]{1,0:T(8,128)(2,1)S(1)} %collective-permute-done.13.rest_14_), channel_id=1, source_target_pairs={{0,16},{1,17},{2,18},{3,19},{4,20},{5,21},{6,22},{7,23},{8,24},{9,... | collective-permute-start | bytes 786440 | tf_op jit(solution)/shard_map/ppermute | solution.py:45
  26.7 9.8 %collective-permute-start.14 = (bf16[128,1024]{1,0:T(8,128)(2,1)S(1)}, bf16[128,1024]{1,0:T(8,128)(2,1)S(1)}, u32[]{:S(2)}, u32[]{:S(2)}) collective-permute-start(bf16[128,1024]{1,0:T(8,128)(2,1)S(1)} %collective-permute-done.13.rest_14_), channel_id=1, source_target_pairs={{0,1},{1,0},{2,3},{3,2},{4,5},{5,4},{6,7},{7,6},{8,9},{9,8},{10,11... | collective-permute-start | bytes 786440 | tf_op jit(solution)/shard_map/ppermute | solution.py:45
  29.3 9.0 %collective-permute-start.19 = (bf16[128,1024]{1,0:T(8,128)(2,1)S(1)}, bf16[128,1024]{1,0:T(8,128)(2,1)}, u32[]{:S(2)}, u32[]{:S(2)}) collective-permute-start(bf16[128,1024]{1,0:T(8,128)(2,1)S(1)} %collective-permute-done.11.rest_12_), channel_id=1, source_target_pairs={{0,2},{1,15},{2,4},{3,1},{4,6},{5,3},{6,8},{7,5},{8,10},{9,7},{10,... | collective-permute-start | bytes 786440 | tf_op jit(solution)/shard_map/ppermute | solution.py:45
  33.4 9.3 %collective-permute-start.15 = (bf16[128,1024]{1,0:T(8,128)(2,1)S(1)}, bf16[128,1024]{1,0:T(8,128)(2,1)S(1)}, u32[]{:S(2)}, u32[]{:S(2)}) collective-permute-start(bf16[128,1024]{1,0:T(8,128)(2,1)S(1)} %collective-permute-done.11.rest_12_), channel_id=1, source_target_pairs={{0,16},{1,17},{2,18},{3,19},{4,20},{5,21},{6,22},{7,23},{8,24},{9,... | collective-permute-start | bytes 786440 | tf_op jit(solution)/shard_map/ppermute | solution.py:45
  33.8 9.5 %collective-permute-start.12 = (bf16[128,1024]{1,0:T(8,128)(2,1)S(1)}, bf16[128,1024]{1,0:T(8,128)(2,1)S(1)}, u32[]{:S(2)}, u32[]{:S(2)}) collective-permute-start(bf16[128,1024]{1,0:T(8,128)(2,1)S(1)} %collective-permute-done.11.rest_12_), channel_id=1, source_target_pairs={{0,1},{1,0},{2,3},{3,2},{4,5},{5,4},{6,7},{7,6},{8,9},{9,8},{10,11... | collective-permute-start | bytes 786440 | tf_op jit(solution)/shard_map/ppermute | solution.py:45
  35.6 9.3 %collective-permute-start.10 = (bf16[128,1024]{1,0:T(8,128)(2,1)S(1)}, bf16[128,1024]{1,0:T(8,128)(2,1)S(1)}, u32[]{:S(2)}, u32[]{:S(2)}) collective-permute-start(bf16[128,1024]{1,0:T(8,128)(2,1)S(1)} %collective-permute-done.9.rest_10_), channel_id=1, source_target_pairs={{0,1},{1,0},{2,3},{3,2},{4,5},{5,4},{6,7},{7,6},{8,9},{9,8},{10,11... | collective-permute-start | bytes 786440 | tf_op jit(solution)/shard_map/ppermute | solution.py:45
  37.2 10.3 %collective-permute-start.8 = (bf16[128,1024]{1,0:T(8,128)(2,1)S(1)}, bf16[128,1024]{1,0:T(8,128)(2,1)S(1)}, u32[]{:S(2)}, u32[]{:S(2)}) collective-permute-start(bf16[128,1024]{1,0:T(8,128)(2,1)S(1)} %collective-permute-done.7.rest_8_), channel_id=1, source_target_pairs={{0,1},{1,0},{2,3},{3,2},{4,5},{5,4},{6,7},{7,6},{8,9},{9,8},{10,11... | collective-permute-start | bytes 786440 | tf_op jit(solution)/shard_map/ppermute | solution.py:45
  38.3 10.1 %collective-permute-start.22 = (bf16[128,1024]{1,0:T(8,128)(2,1)S(1)}, bf16[128,1024]{1,0:T(8,128)(2,1)S(1)}, u32[]{:S(2)}, u32[]{:S(2)}) collective-permute-start(bf16[128,1024]{1,0:T(8,128)(2,1)S(1)} %collective-permute-done.21.rest_22_), channel_id=1, source_target_pairs={{0,1},{1,0},{2,3},{3,2},{4,5},{5,4},{6,7},{7,6},{8,9},{9,8},{10,11... | collective-permute-start | bytes 786440 | tf_op jit(solution)/shard_map/ppermute | solution.py:45
  42.8 7.4 %collective-permute-start.27 = (bf16[128,1024]{1,0:T(8,128)(2,1)}, bf16[128,1024]{1,0:T(8,128)(2,1)}, u32[]{:S(2)}, u32[]{:S(2)}) collective-permute-start(bf16[128,1024]{1,0:T(8,128)(2,1)} %collective-permute-done.19.rest_20_), channel_id=1, source_target_pairs={{0,2},{1,15},{2,4},{3,1},{4,6},{5,3},{6,8},{7,5},{8,10},{9,7},{10,... | collective-permute-start | bytes 786440 | tf_op jit(solution)/shard_map/ppermute | solution.py:45
  44.0 8.8 %collective-permute-start.25 = (bf16[128,1024]{1,0:T(8,128)(2,1)}, bf16[128,1024]{1,0:T(8,128)(2,1)}, u32[]{:S(2)}, u32[]{:S(2)}) collective-permute-start(bf16[128,1024]{1,0:T(8,128)(2,1)} %collective-permute-done.17.rest_18_), channel_id=1, source_target_pairs={{0,14},{1,3},{2,0},{3,5},{4,2},{5,7},{6,4},{7,9},{8,6},{9,11},{10,... | collective-permute-start | bytes 786440 | tf_op jit(solution)/shard_map/ppermute | solution.py:45
  45.6 8.5 %collective-permute-start.18 = (bf16[128,1024]{1,0:T(8,128)(2,1)}, bf16[128,1024]{1,0:T(8,128)(2,1)}, u32[]{:S(2)}, u32[]{:S(2)}) collective-permute-start(bf16[128,1024]{1,0:T(8,128)(2,1)} %collective-permute-done.17.rest_18_), channel_id=1, source_target_pairs={{0,1},{1,0},{2,3},{3,2},{4,5},{5,4},{6,7},{7,6},{8,9},{9,8},{10,11... | collective-permute-start | bytes 786440 | tf_op jit(solution)/shard_map/ppermute | solution.py:45
  48.1 8.3 %collective-permute-start.23 = (bf16[128,1024]{1,0:T(8,128)(2,1)}, bf16[128,1024]{1,0:T(8,128)(2,1)}, u32[]{:S(2)}, u32[]{:S(2)}) collective-permute-start(bf16[128,1024]{1,0:T(8,128)(2,1)} %collective-permute-done.19.rest_20_), channel_id=1, source_target_pairs={{0,16},{1,17},{2,18},{3,19},{4,20},{5,21},{6,22},{7,23},{8,24},{9,... | collective-permute-start | bytes 786440 | tf_op jit(solution)/shard_map/ppermute | solution.py:45
  49.1 8.4 %collective-permute-start.20 = (bf16[128,1024]{1,0:T(8,128)(2,1)}, bf16[128,1024]{1,0:T(8,128)(2,1)}, u32[]{:S(2)}, u32[]{:S(2)}) collective-permute-start(bf16[128,1024]{1,0:T(8,128)(2,1)} %collective-permute-done.19.rest_20_), channel_id=1, source_target_pairs={{0,1},{1,0},{2,3},{3,2},{4,5},{5,4},{6,7},{7,6},{8,9},{9,8},{10,11... | collective-permute-start | bytes 786440 | tf_op jit(solution)/shard_map/ppermute | solution.py:45
  50.1 11.9 %collective-permute-start.29 = (bf16[128,1024]{1,0:T(8,128)(2,1)}, bf16[128,1024]{1,0:T(8,128)(2,1)}, u32[]{:S(2)}, u32[]{:S(2)}) collective-permute-start(bf16[128,1024]{1,0:T(8,128)(2,1)} %collective-permute-done.27.rest_28_), channel_id=1, source_target_pairs={{0,16},{1,17},{2,18},{3,19},{4,20},{5,21},{6,22},{7,23},{8,24},{9,... | collective-permute-start | bytes 786440 | tf_op jit(solution)/shard_map/ppermute | solution.py:45
  52.8 10.9 %collective-permute-start.16 = (bf16[128,1024]{1,0:T(8,128)(2,1)}, bf16[128,1024]{1,0:T(8,128)(2,1)S(1)}, u32[]{:S(2)}, u32[]{:S(2)}) collective-permute-start(bf16[128,1024]{1,0:T(8,128)(2,1)} %copy-done.11), channel_id=1, source_target_pairs={{0,1},{1,0},{2,3},{3,2},{4,5},{5,4},{6,7},{7,6},{8,9},{9,8},{10,11... | collective-permute-start | bytes 786440 | tf_op jit(solution)/shard_map/ppermute | solution.py:45
  54.2 9.5 %collective-permute-start.28 = (bf16[128,1024]{1,0:T(8,128)(2,1)}, bf16[128,1024]{1,0:T(8,128)(2,1)S(1)}, u32[]{:S(2)}, u32[]{:S(2)}) collective-permute-start(bf16[128,1024]{1,0:T(8,128)(2,1)} %collective-permute-done.27.rest_28_), channel_id=1, source_target_pairs={{0,1},{1,0},{2,3},{3,2},{4,5},{5,4},{6,7},{7,6},{8,9},{9,8},{10,11... | collective-permute-start | bytes 786440 | tf_op jit(solution)/shard_map/ppermute | solution.py:45
  56.4 7.3 %collective-permute-start.26 = (bf16[128,1024]{1,0:T(8,128)(2,1)}, bf16[128,1024]{1,0:T(8,128)(2,1)S(1)}, u32[]{:S(2)}, u32[]{:S(2)}) collective-permute-start(bf16[128,1024]{1,0:T(8,128)(2,1)} %collective-permute-done.25.rest_26_), channel_id=1, source_target_pairs={{0,1},{1,0},{2,3},{3,2},{4,5},{5,4},{6,7},{7,6},{8,9},{9,8},{10,11... | collective-permute-start | bytes 786440 | tf_op jit(solution)/shard_map/ppermute | solution.py:45
  57.6 6.1 %collective-permute-start.24 = (bf16[128,1024]{1,0:T(8,128)(2,1)}, bf16[128,1024]{1,0:T(8,128)(2,1)S(1)}, u32[]{:S(2)}, u32[]{:S(2)}) collective-permute-start(bf16[128,1024]{1,0:T(8,128)(2,1)} %collective-permute-done.23.rest_24_), channel_id=1, source_target_pairs={{0,1},{1,0},{2,3},{3,2},{4,5},{5,4},{6,7},{7,6},{8,9},{9,8},{10,11... | collective-permute-start | bytes 786440 | tf_op jit(solution)/shard_map/ppermute | solution.py:45
  62.0 2.2 %collective-permute-start.30 = (bf16[128,1024]{1,0:T(8,128)(2,1)}, bf16[128,1024]{1,0:T(8,128)(2,1)S(1)}, u32[]{:S(2)}, u32[]{:S(2)}) collective-permute-start(bf16[128,1024]{1,0:T(8,128)(2,1)} %collective-permute-done.29.rest_30_), channel_id=1, source_target_pairs={{0,1},{1,0},{2,3},{3,2},{4,5},{5,4},{6,7},{7,6},{8,9},{9,8},{10,11... | collective-permute-start | bytes 786440 | tf_op jit(solution)/shard_map/ppermute | solution.py:45
  (24 other events, 48.3 us)

commit v2 on v0

v2 whole, which is shorter than its diff:
```python
import functools
import math

import jax
import jax.numpy as jnp
from jax import lax
from jax.experimental import pallas as pl
from jax.experimental.pallas import tpu as pltpu
from jax.sharding import PartitionSpec as P

KVH = 4
DH = 128
BS = 128
G = 8
GW = G * DH
ROWS = G * BS
CHUNK = 4
MAXB = 16
CHUNKS = MAXB // CHUNK
MSG = GW + 3 * DH
PLANE = 4
DEPTH = 8
SCALE = DH**-0.5 * math.log2(math.e)


def index(x, z, c):
    return ((x % 2) * 8 + z % 8) * 2 + c % 2


def pairs(target):
    return [
        (index(x, z, c), index(*target(x, z, c)))
        for x in range(2)
        for z in range(8)
        for c in range(2)
    ]


AHEAD = pairs(lambda x, z, c: (x, z + 1 - 2 * c, c))
BACK = pairs(lambda x, z, c: (x, z - 1 + 2 * c, c))
SIBLING = pairs(lambda x, z, c: (x, z, c + 1))
ACROSS = pairs(lambda x, z, c: (x + 1, z, c))
DIAGONAL = pairs(lambda x, z, c: (x + 1, z, c + 1))
PEERS = (SIBLING, ACROSS, DIAGONAL)

VMEM = pl.BlockSpec(memory_space=pltpu.VMEM)
SMEM = pl.BlockSpec(memory_space=pltpu.SMEM)
ANY = pl.BlockSpec(memory_space=pl.ANY)


def send(piece, table):
    return lax.ppermute(piece, "blk", table)


def column(start, size):
    return pl.ds(pl.multiple_of(start * size, size), size)


def pack_pool(head_ref, k_ref, v_ref, *outs):
    for j in range(PLANE):
        head = head_ref[j]
        outs[j][:, :DH] = k_ref[:, column(head, DH)]
        outs[j][:, DH:] = v_ref[:, column(head, DH)]


def pack_request(head_ref, q_ref, k_ref, v_ref, meta_ref, *outs):
    for j in range(PLANE):
        head = head_ref[j]
        outs[j][:, :GW] = q_ref[:, column(head, GW)]
        outs[j][:, GW : GW + DH] = k_ref[:, column(head, DH)]
        outs[j][:, GW + DH : GW + 2 * DH] = v_ref[:, column(head, DH)]
        outs[j][:, GW + 2 * DH :] = meta_ref[...]


def assemble(head_ref, *refs):
    parts, out_ref, sems = refs[:PLANE], refs[PLANE], refs[PLANE + 1]
    copies = [
        pltpu.make_async_copy(parts[j], out_ref.at[:, column(head_ref[j], GW)], sems.at[j])
        for j in range(PLANE)
    ]
    for copy in copies:
        copy.start()
    for copy in copies:
        copy.wait()


def attend(slot_ref, length_ref, *refs):
    msgs, pieces, outs = refs[:2], refs[2 : 2 + DEPTH], refs[2 + DEPTH : 4 + DEPTH]
    kv_ref, qs_ref, s_ref, own_ref, top_ref, acc_ref, sems = refs[4 + DEPTH :]
    copies = [
        pltpu.make_async_copy(pieces[i], kv_ref.at[pl.ds(i * PLANE, PLANE)], sems.at[i])
        for i in range(DEPTH)
    ]
    for copy in copies:
        copy.start()
    row = lax.broadcasted_iota(jnp.int32, (ROWS, BS), 0) % BS
    causal = lax.broadcasted_iota(jnp.int32, (ROWS, BS), 1) <= row
    ones = jnp.ones((BS, DH), jnp.bfloat16)
    count = [(length_ref[r] + CHUNK - 1) // CHUNK for r in range(2)]

    def scores(r, keys):
        return (
            lax.dot_general(
                qs_ref[r], keys, (((1,), (1,)), ((), ())), preferred_element_type=jnp.float32
            )
            * SCALE
        )

    def own_scores(r):
        for h in range(G):
            qs_ref[r, h * BS : (h + 1) * BS, :] = msgs[r][:, h * DH : (h + 1) * DH]
        s = jnp.where(causal, scores(r, msgs[r][:, GW : GW + DH]), -jnp.inf)
        own_ref[r] = s
        top_ref[r] = s

    def entry(r, k, j):
        at = k * CHUNK + j
        live = at < length_ref[r]
        return slot_ref[r, jnp.where(live, at, 0)], live

    def chunk_scores(r, k):
        keys = jnp.concatenate([kv_ref[entry(r, k, j)[0], :, :DH] for j in range(CHUNK)], axis=0)
        s = scores(r, keys)
        s_ref[r, k] = s
        top = top_ref[r]
        for j in range(CHUNK):
            top = jnp.maximum(top, s[:, j * BS : (j + 1) * BS])
        top_ref[r] = top

    def own_values(r):
        top = jnp.broadcast_to(jnp.max(top_ref[r], axis=1, keepdims=True), (ROWS, BS))
        top_ref[r] = top
        w = jnp.exp2(own_ref[r] - top).astype(jnp.bfloat16)
        rhs = jnp.concatenate([msgs[r][:, GW + DH : GW + 2 * DH], ones], axis=1)
        acc_ref[...] = jnp.dot(w, rhs, preferred_element_type=jnp.float32)

    def chunk_values(r, k):
        w = jnp.exp2(s_ref[r, k] - jnp.tile(top_ref[r], (1, CHUNK))).astype(jnp.bfloat16)
        rhs = []
        for j in range(CHUNK):
            slot, live = entry(r, k, j)
            both = jnp.concatenate([kv_ref[slot, :, DH:], ones], axis=1)
            rhs.append(jnp.where(live, both, jnp.zeros_like(both)))
        acc_ref[...] += jnp.dot(w, jnp.concatenate(rhs, axis=0), preferred_element_type=jnp.float32)

    def finish(r):
        for h in range(G):
            a = acc_ref[h * BS : (h + 1) * BS, :]
            outs[r][:, h * DH : (h + 1) * DH] = (a[:, :DH] / a[:, DH:]).astype(jnp.bfloat16)

    own_scores(0)
    for copy in copies:
        copy.wait()

    @pl.loop(0, count[0])
    def _(k):
        chunk_scores(0, k)

    own_values(0)
    own_scores(1)
    both = jnp.minimum(count[0], count[1])

    @pl.loop(0, both)
    def _(k):
        chunk_values(0, k)
        chunk_scores(1, k)

    @pl.loop(both, count[0])
    def _(k):
        chunk_values(0, k)

    @pl.loop(both, count[1])
    def _(k):
        chunk_scores(1, k)

    finish(0)
    own_values(1)

    @pl.loop(0, count[1])
    def _(k):
        chunk_values(1, k)

    finish(1)


def run_attend(slots, lengths, msgs, pieces):
    part = jax.ShapeDtypeStruct((BS, GW), jnp.bfloat16)
    return pl.pallas_call(
        attend,
        out_shape=(part, part),
        in_specs=[SMEM] * 2 + [VMEM] * 2 + [ANY] * DEPTH,
        out_specs=(VMEM, VMEM),
        scratch_shapes=[
            pltpu.VMEM((PLANE * DEPTH, BS, 2 * DH), jnp.bfloat16),
            pltpu.VMEM((2, ROWS, DH), jnp.bfloat16),
            pltpu.VMEM((2, CHUNKS, ROWS, CHUNK * BS), jnp.float32),
            pltpu.VMEM((2, ROWS, BS), jnp.float32),
            pltpu.VMEM((2, ROWS, BS), jnp.float32),
            pltpu.VMEM((ROWS, 2 * DH), jnp.float32),
            pltpu.SemaphoreType.DMA((DEPTH,)),
        ],
        cost_estimate=pl.CostEstimate(flops=2800000000, bytes_accessed=4 << 20, transcendentals=4 << 20),
        compiler_params=pltpu.CompilerParams(vmem_limit_bytes=36 << 20),
    )(slots, lengths, *msgs, *pieces)


def body(queries, new_keys, new_values, prefix_keys, prefix_values, block_table, prefix_blocks):
    me = lax.axis_index("blk")
    x, z, c = me // 16, (me // 2) % 8, me % 2
    heads = jnp.stack([2 * x + c, 2 * x + 1 - c, 2 * (1 - x) + c, 2 * (1 - x) + 1 - c]).astype(jnp.int32)

    shard = jax.ShapeDtypeStruct((BS, 2 * DH), jnp.bfloat16)
    own, *outgoing = pl.pallas_call(
        pack_pool, out_shape=(shard,) * PLANE, in_specs=[SMEM, VMEM, VMEM], out_specs=(VMEM,) * PLANE
    )(heads, prefix_keys, prefix_values)
    piece = jnp.stack([own] + [send(o, t) for o, t in zip(outgoing, PEERS)])

    meta = jnp.concatenate([block_table[0], prefix_blocks]).astype(jnp.bfloat16)
    meta = jnp.broadcast_to(jnp.pad(meta, (0, DH - MAXB - 1))[None], (BS, DH))
    shard = jax.ShapeDtypeStruct((BS, MSG), jnp.bfloat16)
    own, *outgoing = pl.pallas_call(
        pack_request, out_shape=(shard,) * PLANE, in_specs=[SMEM] + [VMEM] * 4, out_specs=(VMEM,) * PLANE
    )(heads, queries, new_keys, new_values, meta)
    msgs = [own] + [send(o, t) for o, t in zip(outgoing, PEERS)]

    a, b = [piece], [piece]
    for step in range(4):
        a.append(send(a[-1], AHEAD))
        if step < 3:
            b.append(send(b[-1], BACK))
    pieces = b + a[:0:-1]

    info = jnp.stack([m[0, GW + 2 * DH : GW + 2 * DH + MAXB + 1] for m in msgs]).astype(jnp.int32)
    table, lengths = info[:, :MAXB], info[:, MAXB]
    deep = (((table // 2) % 8 - z) * (1 - 2 * c)) % 8
    slots = deep * 4 + (table // 16 ^ x) * 2 + (table % 2 ^ c)

    far = run_attend(slots[2:], lengths[2:], msgs[2:], pieces)
    near = run_attend(slots[:2], lengths[:2], msgs[:2], pieces)
    parts = [near[0], send(near[1], SIBLING), send(far[0], ACROSS), send(far[1], DIAGONAL)]
    return pl.pallas_call(
        assemble,
        out_shape=jax.ShapeDtypeStruct(queries.shape, jnp.bfloat16),
        in_specs=[SMEM] + [VMEM] * PLANE,
        out_specs=ANY,
        scratch_shapes=[pltpu.SemaphoreType.DMA((PLANE,))],
    )(heads, *parts)


def solution(mesh):
    spec = P(("grp", "blk"), None)
    return jax.shard_map(
        body, mesh=mesh, in_specs=(spec,) * 6 + (P(("grp", "blk")),), out_specs=spec, check_vma=False
    )
```

time: 449 us -> 89.8 us (0.20); the launches traced: 445 us -> 90 us
  matrix products: 149 us -> 0 us
  waiting for transfers between devices: 125 us -> 39.7 us
  local copies, waits for them, and re-layouts: 64.4 us -> 3.91 us
  loops' own time: 56.5 us -> 0 us
  other arithmetic: 34.9 us -> 1.66 us
  Pallas kernels: 0 us -> 22.9 us
  starting transfers between devices: 0.04 us -> 20.9 us
  between operations: 14.2 us -> 0.9 us
    dot_general x66 -> x0, matrix products: 149 us -> none  [the longest x32 86.5 us: absorb(): jnp.einsum('krl,kld->krd', weights.astype(jnp.bfloat16), value_block, pre...]
    all_gather x2 -> x0, waiting for transfers between devices: 124 us -> none  [the longest x1 67.8 us: body(): piece_values = lax.all_gather(prefix_values, 'blk', axis=0, tiled=True)]
    another operation x1 -> x0, loops' own time: 56.5 us -> none  [body(): state, _ = lax.scan(visit, state, (key_blocks, value_blocks, block_ids))]
    ppermute x0 -> x16, waiting for transfers between devices: none -> 39.7 us  [send(): return lax.ppermute(piece, 'blk', table)]
    dynamic_slice x64 -> x0, local copies, waits for them, and re-layouts: 35.9 us -> none  [the longest x32 18 us: visit(): used[block_id]]
    reduce_sum x33 -> x0, other arithmetic: 33.1 us -> none  [the longest x32 32.6 us: absorb(): total = factor * total + jnp.sum(weights, axis=-1)]
    pallas_call x0 -> x5, Pallas kernels: none -> 22.9 us  [the longest x2 16.4 us: run_attend(): pl.pallas_call(attend, out_shape=(part, part), in_specs=[SMEM] * 2 + [VME...]
    ppermute x0 -> x16, starting transfers between devices: none -> 20.9 us  [send(): return lax.ppermute(piece, 'blk', table)]
  transfers between devices with their start and end apart: 2 -> 16, of which waited for: 2 -> 9; matrix products, arithmetic and copies ran while one was open for 4% -> 2% of each run, Pallas kernels for 0% -> 12%
where the time goes in v2:
time: 89.8 us; the launch traced here: 90 us
  waiting for transfers between devices  39.7 us (44%)
  Pallas kernels  22.9 us (26%)
  starting transfers between devices  20.9 us (23%)
  local copies, waits for them, and re-layouts  3.91 us (4%)
  other arithmetic  1.66 us (2%)
  between operations  0.9 us (1%)
    ppermute x16, waiting for transfers between devices, send(): return lax.ppermute(piece, 'blk', table)  39.7 us
    ppermute x16, starting transfers between devices, send(): return lax.ppermute(piece, 'blk', table)  20.9 us
    pallas_call x2, Pallas kernels, run_attend(): pl.pallas_call(attend, out_shape=(part, part), in_specs=[SMEM] * 2 + [VME...  16.4 us
    pallas_call x1, Pallas kernels, body(): pl.pallas_call(pack_request, out_shape=(shard,) * PLANE, in_specs=[SMEM]...  2.54 us
    unnamed x12, local copies, waits for them, and re-layouts  2.39 us
    pallas_call x1, Pallas kernels, body(): pl.pallas_call(assemble, out_shape=jax.ShapeDtypeStruct(queries.shape, jn...  2.19 us
  transfers between devices with their start and end apart: 16, of which 9 were waited for; matrix products, arithmetic and copies ran while one was open for 2% of the time, Pallas kernels for 12%

profile of v2, /device:TPU:1, one launch (start us, length us, event | category | flops | bytes accessed | tf_op | source)
XLA Modules:
  0.0 90.0 jit_solution(9820138809057797907)
XLA Ops:
  0.0 0.6 pad_add_fusion.head_ref
  0.6 1.7 %shard_map.74 = (bf16[128,256]{1,0:T(8,128)(2,1)}, bf16[128,256]{1,0:T(8,128)(2,1)}, bf16[128,256]{1,0:T(8,128)(2,1)}, bf16[128,256]{1,0:T(8,128)(2,1)}) custom-call(s32[4]{0:T(128)} %pad_add_fusion.head_ref, bf16[128,512]{1,0:T(8,128)(2,1)} %k_ref.3, bf16[128,512]{1,0:T(8,128)(2,1)} %v_ref.3), custom_call_target="tpu_custom_call" | custom-call | tf_op jit(solution)/shard_map/pallas_call | solution.py:213
  2.4 3.2 %collective-permute-start.3 = (bf16[128,256]{1,0:T(8,128)(2,1)}, bf16[128,256]{1,0:T(8,128)(2,1)S(1)}, u32[]{:S(2)}, u32[]{:S(2)}) collective-permute-start(bf16[128,256]{1,0:T(8,128)(2,1)} %get-tuple-element.22), channel_id=1, source_target_pairs={{0,1},{1,0},{2,3},{3,2},{4,5},{5,4},{6,7},{7,6},{8,9},{9,8},{10,11... | collective-permute-start | bytes 196616 | tf_op jit(solution)/shard_map/ppermute | solution.py:52
  5.6 1.7 %collective-permute-start.5 = (bf16[128,256]{1,0:T(8,128)(2,1)}, bf16[128,256]{1,0:T(8,128)(2,1)S(1)}, u32[]{:S(2)}, u32[]{:S(2)}) collective-permute-start(bf16[128,256]{1,0:T(8,128)(2,1)} %get-tuple-element.24), channel_id=1, source_target_pairs={{0,17},{1,16},{2,19},{3,18},{4,21},{5,20},{6,23},{7,22},{8,25},{9,... | collective-permute-start | bytes 196616 | tf_op jit(solution)/shard_map/ppermute | solution.py:52
  7.3 2.2 %collective-permute-done.4 = bf16[128,256]{1,0:T(8,128)(2,1)S(1)} collective-permute-done((bf16[128,256]{1,0:T(8,128)(2,1)}, bf16[128,256]{1,0:T(8,128)(2,1)S(1)}, u32[]{:S(2)}, u32[]{:S(2)}) %collective-permute-start.4) | collective-permute-done | bytes 65568 | tf_op jit(solution)/shard_map/ppermute | solution.py:52
  9.5 1.6 %collective-permute-done.5 = bf16[128,256]{1,0:T(8,128)(2,1)S(1)} collective-permute-done((bf16[128,256]{1,0:T(8,128)(2,1)}, bf16[128,256]{1,0:T(8,128)(2,1)S(1)}, u32[]{:S(2)}, u32[]{:S(2)}) %collective-permute-start.5) | collective-permute-done | bytes 65568 | tf_op jit(solution)/shard_map/ppermute | solution.py:52
  11.0 0.9 pad_maximum_fusion.refs_2_
  11.9 4.0 %collective-permute-start.9 = (bf16[4,128,256]{2,1,0:T(8,128)(2,1)S(1)}, bf16[4,128,256]{2,1,0:T(8,128)(2,1)S(1)}, u32[]{:S(2)}, u32[]{:S(2)}) collective-permute-start(bf16[4,128,256]{2,1,0:T(8,128)(2,1)S(1)} %pad_maximum_fusion.refs_2_), channel_id=1, source_target_pairs={{0,2},{1,15},{2,4},{3,1},{4,6},{5,3},{6,8},{7,5},{8,10},{9,7},{10,... | collective-permute-start | bytes 786440 | tf_op jit(solution)/shard_map/ppermute | solution.py:52
  16.7 0.6 broadcast_in_dim.2.meta_ref
  17.3 2.5 %shard_map.73 = (bf16[128,1408]{1,0:T(8,128)(2,1)}, bf16[128,1408]{1,0:T(8,128)(2,1)}, bf16[128,1408]{1,0:T(8,128)(2,1)}, bf16[128,1408]{1,0:T(8,128)(2,1)}) custom-call(s32[4]{0:T(128)} %pad_add_fusion.head_ref, bf16[128,4096]{1,0:T(8,128)(2,1)} %q_ref.1, bf16[128,512]{1,0:T(8,128)(2,1)} %k_ref.2, bf16[128,512]{1,0:T(8,128)(2,1)} %v_ref.2, ...), custom_call_target="tpu_custom_call" | custom-call | tf_op jit(solution)/shard_map/pallas_call | solution.py:221
  19.8 1.1 %collective-permute-start.1 = (bf16[128,1408]{1,0:T(8,128)(2,1)}, bf16[128,1408]{1,0:T(8,128)(2,1)S(1)}, u32[]{:S(2)}, u32[]{:S(2)}) collective-permute-start(bf16[128,1408]{1,0:T(8,128)(2,1)} %get-tuple-element.19), channel_id=1, source_target_pairs={{0,16},{1,17},{2,18},{3,19},{4,20},{5,21},{6,22},{7,23},{8,24},{9,... | collective-permute-start | bytes 1081352 | tf_op jit(solution)/shard_map/ppermute | solution.py:52
  21.0 1.0 %collective-permute-start.2 = (bf16[128,1408]{1,0:T(8,128)(2,1)}, bf16[128,1408]{1,0:T(8,128)(2,1)S(1)}, u32[]{:S(2)}, u32[]{:S(2)}) collective-permute-start(bf16[128,1408]{1,0:T(8,128)(2,1)} %get-tuple-element.20), channel_id=1, source_target_pairs={{0,17},{1,16},{2,19},{3,18},{4,21},{5,20},{6,23},{7,22},{8,25},{9,... | collective-permute-start | bytes 1081352 | tf_op jit(solution)/shard_map/ppermute | solution.py:52
  22.0 2.7 %collective-permute-start.10 = (bf16[4,128,256]{2,1,0:T(8,128)(2,1)S(1)}, bf16[4,128,256]{2,1,0:T(8,128)(2,1)S(1)}, u32[]{:S(2)}, u32[]{:S(2)}) collective-permute-start(bf16[4,128,256]{2,1,0:T(8,128)(2,1)S(1)} %collective-permute-done.9.refs_9_), channel_id=1, source_target_pairs={{0,2},{1,15},{2,4},{3,1},{4,6},{5,3},{6,8},{7,5},{8,10},{9,7},{10,... | collective-permute-start | bytes 786440 | tf_op jit(solution)/shard_map/ppermute | solution.py:52
  24.6 0.7 slice.36
  25.3 4.9 %collective-permute-done.6.refs_3_ = bf16[4,128,256]{2,1,0:T(8,128)(2,1)S(1)} collective-permute-done((bf16[4,128,256]{2,1,0:T(8,128)(2,1)S(1)}, bf16[4,128,256]{2,1,0:T(8,128)(2,1)S(1)}, u32[]{:S(2)}, u32[]{:S(2)}) %collective-permute-start.6) | collective-permute-done | bytes 262176 | tf_op jit(solution)/shard_map/ppermute | solution.py:52
  30.2 7.7 %collective-permute-done.2.refs_1_ = bf16[128,1408]{1,0:T(8,128)(2,1)S(1)} collective-permute-done((bf16[128,1408]{1,0:T(8,128)(2,1)}, bf16[128,1408]{1,0:T(8,128)(2,1)S(1)}, u32[]{:S(2)}, u32[]{:S(2)}) %collective-permute-start.2) | collective-permute-done | bytes 360480 | tf_op jit(solution)/shard_map/ppermute | solution.py:52
  37.9 0.7 collective-permute-start.11
  38.7 0.8 collective-permute-start.8
  39.5 6.4 %collective-permute-done.11.refs_7_ = bf16[4,128,256]{2,1,0:T(8,128)(2,1)S(1)} collective-permute-done((bf16[4,128,256]{2,1,0:T(8,128)(2,1)S(1)}, bf16[4,128,256]{2,1,0:T(8,128)(2,1)S(1)}, u32[]{:S(2)}, u32[]{:S(2)}) %collective-permute-start.11) | collective-permute-done | bytes 262176 | tf_op jit(solution)/shard_map/ppermute | solution.py:52
  46.1 1.2 %collective-permute-done.8.refs_5_ = bf16[4,128,256]{2,1,0:T(8,128)(2,1)S(1)} collective-permute-done((bf16[4,128,256]{2,1,0:T(8,128)(2,1)S(1)}, bf16[4,128,256]{2,1,0:T(8,128)(2,1)S(1)}, u32[]{:S(2)}, u32[]{:S(2)}) %collective-permute-start.8) | collective-permute-done | bytes 262176 | tf_op jit(solution)/shard_map/ppermute | solution.py:52
  47.3 3.8 %collective-permute-done.12.refs_6_ = bf16[4,128,256]{2,1,0:T(8,128)(2,1)S(1)} collective-permute-done((bf16[4,128,256]{2,1,0:T(8,128)(2,1)S(1)}, bf16[4,128,256]{2,1,0:T(8,128)(2,1)S(1)}, u32[]{:S(2)}, u32[]{:S(2)}) %collective-permute-start.12) | collective-permute-done | bytes 262176 | tf_op jit(solution)/shard_map/ppermute | solution.py:52
  51.1 1.0 %copy-done.1 = bf16[128,1408]{1,0:T(8,128)(2,1)S(1)} copy-done((bf16[128,1408]{1,0:T(8,128)(2,1)S(1)}, bf16[128,1408]{1,0:T(8,128)(2,1)}, u32[]{:S(2)}) %copy-start.1) | copy-done | bytes 360472
  52.1 7.9 %shard_map.75 = (bf16[128,1024]{1,0:T(8,128)(2,1)S(1)}, bf16[128,1024]{1,0:T(8,128)(2,1)S(1)}) custom-call(s32[2,16]{1,0:T(2,128)S(1)} %get-tuple-element.32.slot_ref, s32[2]{0:T(128)S(1)} %get-tuple-element.30.length_ref, bf16[128,1408]{1,0:T(8,128)(2,1)S(1)} %copy-done.1, bf16[128,1408]{1,0:T(8,128)(2,1)S(1)} %collective-permute-done.refs_1_, ...), custom_call_target="tpu_custom_call" | custom-call | flops 2800000000 | bytes 4194304 | tf_op jit(solution)/shard_map/pallas_call | solution.py:188
  60.0 0.7 copy-done
  60.7 3.9 %collective-permute-start.13 = (bf16[128,1024]{1,0:T(8,128)(2,1)S(1)}, bf16[128,1024]{1,0:T(8,128)(2,1)S(1)}, u32[]{:S(2)}, u32[]{:S(2)}) collective-permute-start(bf16[128,1024]{1,0:T(8,128)(2,1)S(1)} %get-tuple-element.26), channel_id=1, source_target_pairs={{0,1},{1,0},{2,3},{3,2},{4,5},{5,4},{6,7},{7,6},{8,9},{9,8},{10,11... | collective-permute-start | bytes 786440 | tf_op jit(solution)/shard_map/ppermute | solution.py:52
  64.7 8.5 %shard_map.76 = (bf16[128,1024]{1,0:T(8,128)(2,1)S(1)}, bf16[128,1024]{1,0:T(8,128)(2,1)S(1)}) custom-call(s32[2,16]{1,0:T(2,128)S(1)} %get-tuple-element.31.slot_ref, s32[2]{0:T(128)S(1)} %get-tuple-element.29.length_ref, bf16[128,1408]{1,0:T(8,128)(2,1)S(1)} %collective-permute-done.1.refs_0_, bf16[128,1408]{1,0:T(8,128)(2,1)S(1)} %collective-permute-done.2.refs_1_, ...), custom_call_target="tpu_custom_call" | custom-call | flops 2800000000 | bytes 4194304 | tf_op jit(solution)/shard_map/pallas_call | solution.py:188
  73.2 1.1 %collective-permute-start.14 = (bf16[128,1024]{1,0:T(8,128)(2,1)S(1)}, bf16[128,1024]{1,0:T(8,128)(2,1)S(1)}, u32[]{:S(2)}, u32[]{:S(2)}) collective-permute-start(bf16[128,1024]{1,0:T(8,128)(2,1)S(1)} %get-tuple-element.27), channel_id=1, source_target_pairs={{0,16},{1,17},{2,18},{3,19},{4,20},{5,21},{6,22},{7,23},{8,24},{9,... | collective-permute-start | bytes 786440 | tf_op jit(solution)/shard_map/ppermute | solution.py:52
  74.3 0.5 collective-permute-start.15
  74.9 6.4 %collective-permute-done.14.refs_2_ = bf16[128,1024]{1,0:T(8,128)(2,1)S(1)} collective-permute-done((bf16[128,1024]{1,0:T(8,128)(2,1)S(1)}, bf16[128,1024]{1,0:T(8,128)(2,1)S(1)}, u32[]{:S(2)}, u32[]{:S(2)}) %collective-permute-start.14) | collective-permute-done | bytes 262176 | tf_op jit(solution)/shard_map/ppermute | solution.py:52
  81.3 5.7 %collective-permute-done.15.refs_3_ = bf16[128,1024]{1,0:T(8,128)(2,1)S(1)} collective-permute-done((bf16[128,1024]{1,0:T(8,128)(2,1)S(1)}, bf16[128,1024]{1,0:T(8,128)(2,1)S(1)}, u32[]{:S(2)}, u32[]{:S(2)}) %collective-permute-start.15) | collective-permute-done | bytes 262176 | tf_op jit(solution)/shard_map/ppermute | solution.py:52
  86.9 0.7 copy-done.4
  87.6 2.2 %shard_map.77 = bf16[128,4096]{1,0:T(8,128)(2,1)} custom-call(s32[4]{0:T(128)} %pad_add_fusion.head_ref, bf16[128,1024]{1,0:T(8,128)(2,1)} %copy-done, bf16[128,1024]{1,0:T(8,128)(2,1)} %copy-done.2, bf16[128,1024]{1,0:T(8,128)(2,1)} %copy-done.3, bf16[128,1024]{1,0:T(8,128)(2,1)} %copy-done.4), custom_call_target="tpu_custom_call" | custom-call | tf_op jit(solution)/shard_map/pallas_call | solution.py:241
  (30 shorter events, 0.4 us)
Async XLA Ops:
  2.4 4.9 %collective-permute-start.3 = (bf16[128,256]{1,0:T(8,128)(2,1)}, bf16[128,256]{1,0:T(8,128)(2,1)S(1)}, u32[]{:S(2)}, u32[]{:S(2)}) collective-permute-start(bf16[128,256]{1,0:T(8,128)(2,1)} %get-tuple-element.22), channel_id=1, source_target_pairs={{0,1},{1,0},{2,3},{3,2},{4,5},{5,4},{6,7},{7,6},{8,9},{9,8},{10,11... | collective-permute-start | bytes 196616 | tf_op jit(solution)/shard_map/ppermute | solution.py:52
  5.6 3.9 %collective-permute-start.4 = (bf16[128,256]{1,0:T(8,128)(2,1)}, bf16[128,256]{1,0:T(8,128)(2,1)S(1)}, u32[]{:S(2)}, u32[]{:S(2)}) collective-permute-start(bf16[128,256]{1,0:T(8,128)(2,1)} %get-tuple-element.23), channel_id=1, source_target_pairs={{0,16},{1,17},{2,18},{3,19},{4,20},{5,21},{6,22},{7,23},{8,24},{9,... | collective-permute-start | bytes 196616 | tf_op jit(solution)/shard_map/ppermute | solution.py:52
  5.6 5.4 %collective-permute-start.5 = (bf16[128,256]{1,0:T(8,128)(2,1)}, bf16[128,256]{1,0:T(8,128)(2,1)S(1)}, u32[]{:S(2)}, u32[]{:S(2)}) collective-permute-start(bf16[128,256]{1,0:T(8,128)(2,1)} %get-tuple-element.24), channel_id=1, source_target_pairs={{0,17},{1,16},{2,19},{3,18},{4,21},{5,20},{6,23},{7,22},{8,25},{9,... | collective-permute-start | bytes 196616 | tf_op jit(solution)/shard_map/ppermute | solution.py:52
  11.0 4.9 %copy-start.5 = (s32[1,16]{1,0:T(1,128)S(1)}, s32[1,16]{1,0:T(1,128)}, u32[]{:S(2)}) copy-start(s32[1,16]{1,0:T(1,128)} %param.12) | copy-start | bytes 196
  11.9 10.0 %collective-permute-start.9 = (bf16[4,128,256]{2,1,0:T(8,128)(2,1)S(1)}, bf16[4,128,256]{2,1,0:T(8,128)(2,1)S(1)}, u32[]{:S(2)}, u32[]{:S(2)}) collective-permute-start(bf16[4,128,256]{2,1,0:T(8,128)(2,1)S(1)} %pad_maximum_fusion.refs_2_), channel_id=1, source_target_pairs={{0,2},{1,15},{2,4},{3,1},{4,6},{5,3},{6,8},{7,5},{8,10},{9,7},{10,... | collective-permute-start | bytes 786440 | tf_op jit(solution)/shard_map/ppermute | solution.py:52
  19.8 10.4 %collective-permute-start = (bf16[128,1408]{1,0:T(8,128)(2,1)}, bf16[128,1408]{1,0:T(8,128)(2,1)S(1)}, u32[]{:S(2)}, u32[]{:S(2)}) collective-permute-start(bf16[128,1408]{1,0:T(8,128)(2,1)} %get-tuple-element.18), channel_id=1, source_target_pairs={{0,1},{1,0},{2,3},{3,2},{4,5},{5,4},{6,7},{7,6},{8,9},{9,8},{10,11... | collective-permute-start | bytes 1081352 | tf_op jit(solution)/shard_map/ppermute | solution.py:52
  19.8 10.4 %collective-permute-start.1 = (bf16[128,1408]{1,0:T(8,128)(2,1)}, bf16[128,1408]{1,0:T(8,128)(2,1)S(1)}, u32[]{:S(2)}, u32[]{:S(2)}) collective-permute-start(bf16[128,1408]{1,0:T(8,128)(2,1)} %get-tuple-element.19), channel_id=1, source_target_pairs={{0,16},{1,17},{2,18},{3,19},{4,20},{5,21},{6,22},{7,23},{8,24},{9,... | collective-permute-start | bytes 1081352 | tf_op jit(solution)/shard_map/ppermute | solution.py:52
  21.0 16.9 %collective-permute-start.2 = (bf16[128,1408]{1,0:T(8,128)(2,1)}, bf16[128,1408]{1,0:T(8,128)(2,1)S(1)}, u32[]{:S(2)}, u32[]{:S(2)}) collective-permute-start(bf16[128,1408]{1,0:T(8,128)(2,1)} %get-tuple-element.20), channel_id=1, source_target_pairs={{0,17},{1,16},{2,19},{3,18},{4,21},{5,20},{6,23},{7,22},{8,25},{9,... | collective-permute-start | bytes 1081352 | tf_op jit(solution)/shard_map/ppermute | solution.py:52
  22.0 8.2 %collective-permute-start.6 = (bf16[4,128,256]{2,1,0:T(8,128)(2,1)S(1)}, bf16[4,128,256]{2,1,0:T(8,128)(2,1)S(1)}, u32[]{:S(2)}, u32[]{:S(2)}) collective-permute-start(bf16[4,128,256]{2,1,0:T(8,128)(2,1)S(1)} %pad_maximum_fusion.refs_2_), channel_id=1, source_target_pairs={{0,14},{1,3},{2,0},{3,5},{4,2},{5,7},{6,4},{7,9},{8,6},{9,11},{10,... | collective-permute-start | bytes 786440 | tf_op jit(solution)/shard_map/ppermute | solution.py:52
  22.0 15.9 %collective-permute-start.10 = (bf16[4,128,256]{2,1,0:T(8,128)(2,1)S(1)}, bf16[4,128,256]{2,1,0:T(8,128)(2,1)S(1)}, u32[]{:S(2)}, u32[]{:S(2)}) collective-permute-start(bf16[4,128,256]{2,1,0:T(8,128)(2,1)S(1)} %collective-permute-done.9.refs_9_), channel_id=1, source_target_pairs={{0,2},{1,15},{2,4},{3,1},{4,6},{5,3},{6,8},{7,5},{8,10},{9,7},{10,... | collective-permute-start | bytes 786440 | tf_op jit(solution)/shard_map/ppermute | solution.py:52
  30.2 8.5 %collective-permute-start.7 = (bf16[4,128,256]{2,1,0:T(8,128)(2,1)S(1)}, bf16[4,128,256]{2,1,0:T(8,128)(2,1)S(1)}, u32[]{:S(2)}, u32[]{:S(2)}) collective-permute-start(bf16[4,128,256]{2,1,0:T(8,128)(2,1)S(1)} %collective-permute-done.6.refs_3_), channel_id=1, source_target_pairs={{0,14},{1,3},{2,0},{3,5},{4,2},{5,7},{6,4},{7,9},{8,6},{9,11},{10,... | collective-permute-start | bytes 786440 | tf_op jit(solution)/shard_map/ppermute | solution.py:52
  37.9 8.0 %collective-permute-start.11 = (bf16[4,128,256]{2,1,0:T(8,128)(2,1)S(1)}, bf16[4,128,256]{2,1,0:T(8,128)(2,1)S(1)}, u32[]{:S(2)}, u32[]{:S(2)}) collective-permute-start(bf16[4,128,256]{2,1,0:T(8,128)(2,1)S(1)} %collective-permute-done.10.refs_8_), channel_id=1, source_target_pairs={{0,2},{1,15},{2,4},{3,1},{4,6},{5,3},{6,8},{7,5},{8,10},{9,7},{10,... | collective-permute-start | bytes 786440 | tf_op jit(solution)/shard_map/ppermute | solution.py:52
  38.7 8.7 %collective-permute-start.8 = (bf16[4,128,256]{2,1,0:T(8,128)(2,1)S(1)}, bf16[4,128,256]{2,1,0:T(8,128)(2,1)S(1)}, u32[]{:S(2)}, u32[]{:S(2)}) collective-permute-start(bf16[4,128,256]{2,1,0:T(8,128)(2,1)S(1)} %collective-permute-done.7.refs_4_), channel_id=1, source_target_pairs={{0,14},{1,3},{2,0},{3,5},{4,2},{5,7},{6,4},{7,9},{8,6},{9,11},{10,... | collective-permute-start | bytes 786440 | tf_op jit(solution)/shard_map/ppermute | solution.py:52
  45.9 5.2 %collective-permute-start.12 = (bf16[4,128,256]{2,1,0:T(8,128)(2,1)S(1)}, bf16[4,128,256]{2,1,0:T(8,128)(2,1)S(1)}, u32[]{:S(2)}, u32[]{:S(2)}) collective-permute-start(bf16[4,128,256]{2,1,0:T(8,128)(2,1)S(1)} %collective-permute-done.11.refs_7_), channel_id=1, source_target_pairs={{0,2},{1,15},{2,4},{3,1},{4,6},{5,3},{6,8},{7,5},{8,10},{9,7},{10,... | collective-permute-start | bytes 786440 | tf_op jit(solution)/shard_map/ppermute | solution.py:52
  51.1 1.0 %copy-start.1 = (bf16[128,1408]{1,0:T(8,128)(2,1)S(1)}, bf16[128,1408]{1,0:T(8,128)(2,1)}, u32[]{:S(2)}) copy-start(bf16[128,1408]{1,0:T(8,128)(2,1)} %get-tuple-element.17.refs_0_) | copy-start | bytes 1081348
  60.0 0.7 copy-start
  60.7 14.1 %collective-permute-start.13 = (bf16[128,1024]{1,0:T(8,128)(2,1)S(1)}, bf16[128,1024]{1,0:T(8,128)(2,1)S(1)}, u32[]{:S(2)}, u32[]{:S(2)}) collective-permute-start(bf16[128,1024]{1,0:T(8,128)(2,1)S(1)} %get-tuple-element.26), channel_id=1, source_target_pairs={{0,1},{1,0},{2,3},{3,2},{4,5},{5,4},{6,7},{7,6},{8,9},{9,8},{10,11... | collective-permute-start | bytes 786440 | tf_op jit(solution)/shard_map/ppermute | solution.py:52
  73.2 8.1 %collective-permute-start.14 = (bf16[128,1024]{1,0:T(8,128)(2,1)S(1)}, bf16[128,1024]{1,0:T(8,128)(2,1)S(1)}, u32[]{:S(2)}, u32[]{:S(2)}) collective-permute-start(bf16[128,1024]{1,0:T(8,128)(2,1)S(1)} %get-tuple-element.27), channel_id=1, source_target_pairs={{0,16},{1,17},{2,18},{3,19},{4,20},{5,21},{6,22},{7,23},{8,24},{9,... | collective-permute-start | bytes 786440 | tf_op jit(solution)/shard_map/ppermute | solution.py:52
  74.3 12.6 %collective-permute-start.15 = (bf16[128,1024]{1,0:T(8,128)(2,1)S(1)}, bf16[128,1024]{1,0:T(8,128)(2,1)S(1)}, u32[]{:S(2)}, u32[]{:S(2)}) collective-permute-start(bf16[128,1024]{1,0:T(8,128)(2,1)S(1)} %get-tuple-element.28), channel_id=1, source_target_pairs={{0,17},{1,16},{2,19},{3,18},{4,21},{5,20},{6,23},{7,22},{8,25},{9,... | collective-permute-start | bytes 786440 | tf_op jit(solution)/shard_map/ppermute | solution.py:52
  74.9 12.1 %copy-start.2 = (bf16[128,1024]{1,0:T(8,128)(2,1)}, bf16[128,1024]{1,0:T(8,128)(2,1)S(1)}, u32[]{:S(2)}) copy-start(bf16[128,1024]{1,0:T(8,128)(2,1)S(1)} %collective-permute-done.13.refs_1_) | copy-start | bytes 786436
  81.3 5.7 %copy-start.3 = (bf16[128,1024]{1,0:T(8,128)(2,1)}, bf16[128,1024]{1,0:T(8,128)(2,1)S(1)}, u32[]{:S(2)}) copy-start(bf16[128,1024]{1,0:T(8,128)(2,1)S(1)} %collective-permute-done.14.refs_2_) | copy-start | bytes 786436
  86.9 0.7 copy-start.4

commit v3 on v2

--- a/solution.py
+++ b/solution.py
@@ -20,6 +20,8 @@
 MSG = GW + 3 * DH
 PLANE = 4
 DEPTH = 8
+PIECES = 2 * DEPTH
+HALF = PLANE // 2
 SCALE = DH**-0.5 * math.log2(math.e)
 
 
@@ -72,31 +74,36 @@
         outs[j][:, GW + 2 * DH :] = meta_ref[...]
 
 
-def assemble(head_ref, *refs):
-    parts, out_ref, sems = refs[:PLANE], refs[PLANE], refs[PLANE + 1]
+def assemble(cuts, head_ref, *refs):
+    total = sum(cuts)
+    parts, out_ref, sems = refs[:total], refs[total], refs[total + 1]
+    copies = []
+    for j in range(PLANE):
+        rows = BS // cuts[j]
+        for i in range(cuts[j]):
+            target = out_ref.at[i * rows : (i + 1) * rows, column(head_ref[j], GW)]
+            at = len(copies)
+            copies.append(pltpu.make_async_copy(parts[at].at[:rows], target, sems.at[at]))
+    for copy in copies:
+        copy.start()
+    for copy in copies:
+        copy.wait()
+
+
+def attend(cuts, slot_ref, length_ref, *refs):
+    n, total = len(cuts), sum(cuts)
+    msgs, pieces, outs = refs[:n], refs[n : n + PIECES], refs[n + PIECES : n + PIECES + total]
+    kv_ref, qs_ref, s_ref, own_ref, top_ref, acc_ref, sems = refs[n + PIECES + total :]
     copies = [
-        pltpu.make_async_copy(parts[j], out_ref.at[:, column(head_ref[j], GW)], sems.at[j])
-        for j in range(PLANE)
-    ]
-    for copy in copies:
-        copy.start()
-    for copy in copies:
-        copy.wait()
-
-
-def attend(slot_ref, length_ref, *refs):
-    msgs, pieces, outs = refs[:2], refs[2 : 2 + DEPTH], refs[2 + DEPTH : 4 + DEPTH]
-    kv_ref, qs_ref, s_ref, own_ref, top_ref, acc_ref, sems = refs[4 + DEPTH :]
-    copies = [
-        pltpu.make_async_copy(pieces[i], kv_ref.at[pl.ds(i * PLANE, PLANE)], sems.at[i])
-        for i in range(DEPTH)
+        pltpu.make_async_copy(pieces[i], kv_ref.at[pl.ds(i * HALF, HALF)], sems.at[i])
+        for i in range(PIECES)
     ]
     for copy in copies:
         copy.start()
     row = lax.broadcasted_iota(jnp.int32, (ROWS, BS), 0) % BS
     causal = lax.broadcasted_iota(jnp.int32, (ROWS, BS), 1) <= row
     ones = jnp.ones((BS, DH), jnp.bfloat16)
-    count = [(length_ref[r] + CHUNK - 1) // CHUNK for r in range(2)]
+    count = [(length_ref[r] + CHUNK - 1) // CHUNK for r in range(n)]
 
     def scores(r, keys):
         return (
@@ -146,8 +153,14 @@
     def finish(r):
         for h in range(G):
             a = acc_ref[h * BS : (h + 1) * BS, :]
-            outs[r][:, h * DH : (h + 1) * DH] = (a[:, :DH] / a[:, DH:]).astype(jnp.bfloat16)
-
+            a = (a[:, :DH] / a[:, DH:]).astype(jnp.bfloat16)
+            rows = BS // cuts[r]
+            for i in range(cuts[r]):
+                outs[sum(cuts[:r]) + i][:rows, h * DH : (h + 1) * DH] = a[i * rows : (i + 1) * rows]
+
+    for out in outs:
+        if out.shape[0] > BS:
+            out[BS:] = jnp.zeros_like(out[BS:])
     own_scores(0)
     for copy in copies:
         copy.wait()
@@ -156,51 +169,52 @@
     def _(k):
         chunk_scores(0, k)
 
-    own_values(0)
-    own_scores(1)
-    both = jnp.minimum(count[0], count[1])
-
-    @pl.loop(0, both)
-    def _(k):
-        chunk_values(0, k)
-        chunk_scores(1, k)
-
-    @pl.loop(both, count[0])
-    def _(k):
-        chunk_values(0, k)
-
-    @pl.loop(both, count[1])
-    def _(k):
-        chunk_scores(1, k)
-
-    finish(0)
-    own_values(1)
-
-    @pl.loop(0, count[1])
-    def _(k):
-        chunk_values(1, k)
-
-    finish(1)
-
-
-def run_attend(slots, lengths, msgs, pieces):
-    part = jax.ShapeDtypeStruct((BS, GW), jnp.bfloat16)
+    for r in range(n):
+        own_values(r)
+        if r + 1 < n:
+            own_scores(r + 1)
+            both = jnp.minimum(count[r], count[r + 1])
+
+            @pl.loop(0, both)
+            def _(k, r=r):
+                chunk_values(r, k)
+                chunk_scores(r + 1, k)
+
+            @pl.loop(both, count[r])
+            def _(k, r=r):
+                chunk_values(r, k)
+
+            @pl.loop(both, count[r + 1])
+            def _(k, r=r):
+                chunk_scores(r + 1, k)
+        else:
+
+            @pl.loop(0, count[r])
+            def _(k, r=r):
+                chunk_values(r, k)
+
+        finish(r)
+
+
+def run_attend(slots, lengths, msgs, pieces, cuts, extra=0):
+    n = len(msgs)
+    parts = [jax.ShapeDtypeStruct((BS // cut + extra, GW), jnp.bfloat16) for cut in cuts for _ in range(cut)]
     return pl.pallas_call(
-        attend,
-        out_shape=(part, part),
-        in_specs=[SMEM] * 2 + [VMEM] * 2 + [ANY] * DEPTH,
-        out_specs=(VMEM, VMEM),
+        functools.partial(attend, cuts),
+        out_shape=parts,
+        in_specs=[SMEM] * 2 + [VMEM] * n + [ANY] * PIECES,
+        out_specs=[VMEM] * len(parts),
         scratch_shapes=[
             pltpu.VMEM((PLANE * DEPTH, BS, 2 * DH), jnp.bfloat16),
-            pltpu.VMEM((2, ROWS, DH), jnp.bfloat16),
-            pltpu.VMEM((2, CHUNKS, ROWS, CHUNK * BS), jnp.float32),
-            pltpu.VMEM((2, ROWS, BS), jnp.float32),
-            pltpu.VMEM((2, ROWS, BS), jnp.float32),
+            pltpu.VMEM((n, ROWS, DH), jnp.bfloat16),
+            pltpu.VMEM((n, CHUNKS, ROWS, CHUNK * BS), jnp.float32),
+            pltpu.VMEM((n, ROWS, BS), jnp.float32),
+            pltpu.VMEM((n, ROWS, BS), jnp.float32),
             pltpu.VMEM((ROWS, 2 * DH), jnp.float32),
-            pltpu.SemaphoreType.DMA((DEPTH,)),
+            pltpu.SemaphoreType.DMA((PIECES,)),
         ],
-        cost_estimate=pl.CostEstimate(flops=2800000000, bytes_accessed=4 << 20, transcendentals=4 << 20),
-        compiler_params=pltpu.CompilerParams(vmem_limit_bytes=36 << 20),
+        cost_estimate=pl.CostEstimate(flops=1, bytes_accessed=1, transcendentals=1),
+        compiler_params=pltpu.CompilerParams(vmem_limit_bytes=(12 + 12 * n) << 20),
     )(slots, lengths, *msgs, *pieces)
 
 
@@ -211,40 +225,54 @@
 
     shard = jax.ShapeDtypeStruct((BS, 2 * DH), jnp.bfloat16)
     own, *outgoing = pl.pallas_call(
-        pack_pool, out_shape=(shard,) * PLANE, in_specs=[SMEM, VMEM, VMEM], out_specs=(VMEM,) * PLANE
+        pack_pool, out_shape=(shard,) * PLANE, in_specs=[SMEM, VMEM, VMEM], out_specs=(VMEM,) * PLANE,
+        compiler_params=pltpu.CompilerParams(vmem_limit_bytes=8 << 20),
     )(heads, prefix_keys, prefix_values)
-    piece = jnp.stack([own] + [send(o, t) for o, t in zip(outgoing, PEERS)])
+    arrived = [own] + [send(o, t) for o, t in zip(outgoing, PEERS)]
+    first, second = jnp.stack(arrived[:HALF]), jnp.stack(arrived[HALF:])
 
     meta = jnp.concatenate([block_table[0], prefix_blocks]).astype(jnp.bfloat16)
     meta = jnp.broadcast_to(jnp.pad(meta, (0, DH - MAXB - 1))[None], (BS, DH))
     shard = jax.ShapeDtypeStruct((BS, MSG), jnp.bfloat16)
     own, *outgoing = pl.pallas_call(
-        pack_request, out_shape=(shard,) * PLANE, in_specs=[SMEM] + [VMEM] * 4, out_specs=(VMEM,) * PLANE
+        pack_request, out_shape=(shard,) * PLANE, in_specs=[SMEM] + [VMEM] * 4, out_specs=(VMEM,) * PLANE,
+        compiler_params=pltpu.CompilerParams(vmem_limit_bytes=8 << 20),
     )(heads, queries, new_keys, new_values, meta)
     msgs = [own] + [send(o, t) for o, t in zip(outgoing, PEERS)]
 
-    a, b = [piece], [piece]
+    a, b = [(first, second)], [(first, second)]
     for step in range(4):
-        a.append(send(a[-1], AHEAD))
+        a.append(tuple(send(p, AHEAD) for p in a[-1]))
         if step < 3:
-            b.append(send(b[-1], BACK))
-    pieces = b + a[:0:-1]
+            b.append(tuple(send(p, BACK) for p in b[-1]))
+    pieces = [p for both in b + a[:0:-1] for p in both]
+    msgs, pieces = lax.optimization_barrier((msgs, pieces))
 
     info = jnp.stack([m[0, GW + 2 * DH : GW + 2 * DH + MAXB + 1] for m in msgs]).astype(jnp.int32)
     table, lengths = info[:, :MAXB], info[:, MAXB]
     deep = (((table // 2) % 8 - z) * (1 - 2 * c)) % 8
     slots = deep * 4 + (table // 16 ^ x) * 2 + (table % 2 ^ c)
 
-    far = run_attend(slots[2:], lengths[2:], msgs[2:], pieces)
-    near = run_attend(slots[:2], lengths[:2], msgs[:2], pieces)
-    parts = [near[0], send(near[1], SIBLING), send(far[0], ACROSS), send(far[1], DIAGONAL)]
+    across = run_attend(slots[2:3], lengths[2:3], msgs[2:3], pieces, (1,), extra=16)
+    late, _ = lax.optimization_barrier((msgs[3], across))
+    diagonal = run_attend(slots[3:], lengths[3:], [late], pieces, (1,))
+    late, _ = lax.optimization_barrier((msgs[1], diagonal))
+    *sibling, mine = run_attend(slots[1::-1], lengths[1::-1], [late, msgs[0]], pieces, (2, 1))
+    parts = [
+        [mine],
+        [send(p, SIBLING) for p in sibling],
+        [send(p, ACROSS) for p in across],
+        [send(p, DIAGONAL) for p in diagonal],
+    ]
+    cuts = tuple(len(p) for p in parts)
     return pl.pallas_call(
-        assemble,
+        functools.partial(assemble, cuts),
         out_shape=jax.ShapeDtypeStruct(queries.shape, jnp.bfloat16),
-        in_specs=[SMEM] + [VMEM] * PLANE,
+        in_specs=[SMEM] + [VMEM] * sum(cuts),
         out_specs=ANY,
-        scratch_shapes=[pltpu.SemaphoreType.DMA((PLANE,))],
-    )(heads, *parts)
+        scratch_shapes=[pltpu.SemaphoreType.DMA((sum(cuts),))],
+        compiler_params=pltpu.CompilerParams(vmem_limit_bytes=8 << 20),
+    )(heads, *[p for group in parts for p in group])
 
 
 def solution(mesh):

time: 89.8 us -> 82.4 us (0.918)
  waiting for transfers between devices: 39.7 us -> 12.8 us
  starting transfers between devices: 20.9 us -> 32.5 us
  Pallas kernels: 22.9 us -> 32.8 us
  other arithmetic: 1.66 us -> 0.23 us
    ppermute x16 -> x24, waiting for transfers between devices: 39.7 us -> 12.8 us  [send(): return lax.ppermute(piece, 'blk', table)]
    pallas_call x3 -> x4, Pallas kernels: 18.6 us -> 30.8 us  [the longest x3 29.3 us: run_attend(): pl.pallas_call(functools.partial(attend, cuts), out_shape=parts, in_specs...]
    ppermute x16 -> x24, starting transfers between devices: 20.9 us -> 32.5 us  [send(): return lax.ppermute(piece, 'blk', table)]
    pallas_call x1, Pallas kernels: 2.54 us -> 1.4 us  [body(): pl.pallas_call(pack_request, out_shape=(shard,) * PLANE, in_specs=[SMEM]...]
    pallas_call x1, Pallas kernels: 1.72 us -> 0.59 us  [body(): pl.pallas_call(pack_pool, out_shape=(shard,) * PLANE, in_specs=[SMEM, VME...]
  transfers between devices with their start and end apart: 16 -> 24, of which waited for: 9 -> 8; matrix products, arithmetic and copies ran while one was open for 2% -> 1% of each run, Pallas kernels for 12% -> 26%
where the time goes in v3:
time: 82.4 us; the launch traced here: 83.3 us
  Pallas kernels  32.8 us (40%)
  starting transfers between devices  32.5 us (39%)
  waiting for transfers between devices  12.8 us (16%)
  local copies, waits for them, and re-layouts  3.95 us (5%)
  between operations  0.95 us (1%)
    ppermute x24, starting transfers between devices, send(): return lax.ppermute(piece, 'blk', table)  32.5 us
    pallas_call x3, Pallas kernels, run_attend(): pl.pallas_call(functools.partial(attend, cuts), out_shape=parts, in_specs...  29.3 us
    ppermute x24, waiting for transfers between devices, send(): return lax.ppermute(piece, 'blk', table)  12.8 us
    unnamed x12, local copies, waits for them, and re-layouts  3.04 us
  transfers between devices with their start and end apart: 24, of which 8 were waited for; matrix products, arithmetic and copies ran while one was open for 1% of the time, Pallas kernels for 26%

profile of v3, /device:TPU:1, one launch (start us, length us, event | category | flops | bytes accessed | tf_op | source)
XLA Modules:
  0.0 83.3 jit_solution(15794331100366614058)
XLA Ops:
  0.1 0.9 %copy-done.3 = bf16[128,512]{1,0:T(8,128)(2,1)S(1)} copy-done((bf16[128,512]{1,0:T(8,128)(2,1)S(1)}, bf16[128,512]{1,0:T(8,128)(2,1)}, u32[]{:S(2)}) %copy-start.3) | copy-done | bytes 131096
  1.0 0.9 %copy-done.4 = bf16[128,512]{1,0:T(8,128)(2,1)S(1)} copy-done((bf16[128,512]{1,0:T(8,128)(2,1)S(1)}, bf16[128,512]{1,0:T(8,128)(2,1)}, u32[]{:S(2)}) %copy-start.4) | copy-done | bytes 131096
  1.9 0.6 shard_map.74
  2.5 2.1 %collective-permute-start.4 = (bf16[128,256]{1,0:T(8,128)(2,1)S(1)}, bf16[128,256]{1,0:T(8,128)(2,1)S(1)}, u32[]{:S(2)}, u32[]{:S(2)}) collective-permute-start(bf16[128,256]{1,0:T(8,128)(2,1)S(1)} %get-tuple-element.44), channel_id=1, source_target_pairs={{0,16},{1,17},{2,18},{3,19},{4,20},{5,21},{6,22},{7,23},{8,24},{9,... | collective-permute-start | bytes 196616 | tf_op jit(solution)/shard_map/ppermute | solution.py:54
  4.6 2.8 %collective-permute-start.5 = (bf16[128,256]{1,0:T(8,128)(2,1)S(1)}, bf16[128,256]{1,0:T(8,128)(2,1)S(1)}, u32[]{:S(2)}, u32[]{:S(2)}) collective-permute-start(bf16[128,256]{1,0:T(8,128)(2,1)S(1)} %get-tuple-element.45), channel_id=1, source_target_pairs={{0,17},{1,16},{2,19},{3,18},{4,21},{5,20},{6,23},{7,22},{8,25},{9,... | collective-permute-start | bytes 196616 | tf_op jit(solution)/shard_map/ppermute | solution.py:54
  7.5 2.9 %collective-permute-done.5 = bf16[128,256]{1,0:T(8,128)(2,1)S(1)} collective-permute-done((bf16[128,256]{1,0:T(8,128)(2,1)S(1)}, bf16[128,256]{1,0:T(8,128)(2,1)S(1)}, u32[]{:S(2)}, u32[]{:S(2)}) %collective-permute-start.5) | collective-permute-done | bytes 65568 | tf_op jit(solution)/shard_map/ppermute | solution.py:54
  10.3 4.5 %collective-permute-start.16 = (bf16[2,128,256]{2,1,0:T(8,128)(2,1)S(1)}, bf16[2,128,256]{2,1,0:T(8,128)(2,1)S(1)}, u32[]{:S(2)}, u32[]{:S(2)}) collective-permute-start(bf16[2,128,256]{2,1,0:T(8,128)(2,1)S(1)} %pad_maximum_fusion.1.refs_2_.refs_3_), channel_id=1, source_target_pairs={{0,2},{1,15},{2,4},{3,1},{4,6},{5,3},{6,8},{7,5},{8,10},{9,7},{10,... | collective-permute-start | bytes 393224 | tf_op jit(solution)/shard_map/ppermute | solution.py:54
  14.9 2.7 %collective-permute-start.12 = (bf16[2,128,256]{2,1,0:T(8,128)(2,1)S(1)}, bf16[2,128,256]{2,1,0:T(8,128)(2,1)S(1)}, u32[]{:S(2)}, u32[]{:S(2)}) collective-permute-start(bf16[2,128,256]{2,1,0:T(8,128)(2,1)S(1)} %pad_maximum_fusion.refs_1_.refs_2_), channel_id=1, source_target_pairs={{0,2},{1,15},{2,4},{3,1},{4,6},{5,3},{6,8},{7,5},{8,10},{9,7},{10,... | collective-permute-start | bytes 393224 | tf_op jit(solution)/shard_map/ppermute | solution.py:54
  18.4 2.7 %collective-permute-start.17 = (bf16[2,128,256]{2,1,0:T(8,128)(2,1)S(1)}, bf16[2,128,256]{2,1,0:T(8,128)(2,1)S(1)}, u32[]{:S(2)}, u32[]{:S(2)}) collective-permute-start(bf16[2,128,256]{2,1,0:T(8,128)(2,1)S(1)} %collective-permute-done.16.refs_16_.refs_17_), channel_id=1, source_target_pairs={{0,2},{1,15},{2,4},{3,1},{4,6},{5,3},{6,8},{7,5},{8,10},{9,7},{10,... | collective-permute-start | bytes 393224 | tf_op jit(solution)/shard_map/ppermute | solution.py:54
  21.1 1.2 %copy-done = bf16[128,4096]{1,0:T(8,128)(2,1)S(1)} copy-done((bf16[128,4096]{1,0:T(8,128)(2,1)S(1)}, bf16[128,4096]{1,0:T(8,128)(2,1)}, u32[]{:S(2)}) %copy-start) | copy-done | bytes 1048600
  22.4 1.4 %shard_map.73 = (bf16[128,1408]{1,0:T(8,128)(2,1)S(1)}, bf16[128,1408]{1,0:T(8,128)(2,1)S(1)}, bf16[128,1408]{1,0:T(8,128)(2,1)S(1)}, bf16[128,1408]{1,0:T(8,128)(2,1)}) custom-call(s32[4]{0:T(128)S(1)} %pad_add_fusion.head_ref, bf16[128,4096]{1,0:T(8,128)(2,1)S(1)} %copy-done, bf16[128,512]{1,0:T(8,128)(2,1)S(1)} %copy-done.1, ...), custom_call_target="tpu_custom_call" | custom-call | tf_op jit(solution)/shard_map/pallas_call | solution.py:237
  23.8 1.8 %collective-permute-start.13 = (bf16[2,128,256]{2,1,0:T(8,128)(2,1)S(1)}, bf16[2,128,256]{2,1,0:T(8,128)(2,1)S(1)}, u32[]{:S(2)}, u32[]{:S(2)}) collective-permute-start(bf16[2,128,256]{2,1,0:T(8,128)(2,1)S(1)} %collective-permute-done.12.refs_15_.refs_16_), channel_id=1, source_target_pairs={{0,2},{1,15},{2,4},{3,1},{4,6},{5,3},{6,8},{7,5},{8,10},{9,7},{10,... | collective-permute-start | bytes 393224 | tf_op jit(solution)/shard_map/ppermute | solution.py:54
  25.6 0.5 collective-permute-start.1
  26.1 0.3 collective-permute-start.9
  26.5 1.4 %collective-permute-done.13.refs_13_.refs_14_ = bf16[2,128,256]{2,1,0:T(8,128)(2,1)S(1)} collective-permute-done((bf16[2,128,256]{2,1,0:T(8,128)(2,1)S(1)}, bf16[2,128,256]{2,1,0:T(8,128)(2,1)S(1)}, u32[]{:S(2)}, u32[]{:S(2)}) %collective-permute-start.13) | collective-permute-done | bytes 131104 | tf_op jit(solution)/shard_map/ppermute | solution.py:54
  27.9 3.8 %collective-permute-start.2 = (bf16[128,1408]{1,0:T(8,128)(2,1)}, bf16[128,1408]{1,0:T(8,128)(2,1)S(1)}, u32[]{:S(2)}, u32[]{:S(2)}) collective-permute-start(bf16[128,1408]{1,0:T(8,128)(2,1)} %get-tuple-element.41), channel_id=1, source_target_pairs={{0,17},{1,16},{2,19},{3,18},{4,21},{5,20},{6,23},{7,22},{8,25},{9,... | collective-permute-start | bytes 1081352 | tf_op jit(solution)/shard_map/ppermute | solution.py:54
  31.7 0.8 %collective-permute-done.8.refs_5_.refs_6_ = bf16[2,128,256]{2,1,0:T(8,128)(2,1)S(1)} collective-permute-done((bf16[2,128,256]{2,1,0:T(8,128)(2,1)S(1)}, bf16[2,128,256]{2,1,0:T(8,128)(2,1)S(1)}, u32[]{:S(2)}, u32[]{:S(2)}) %collective-permute-start.8) | collective-permute-done | bytes 131104 | tf_op jit(solution)/shard_map/ppermute | solution.py:54
  32.6 0.4 collective-permute-start.14
  33.0 1.1 %collective-permute-start.11 = (bf16[2,128,256]{2,1,0:T(8,128)(2,1)S(1)}, bf16[2,128,256]{2,1,0:T(8,128)(2,1)S(1)}, u32[]{:S(2)}, u32[]{:S(2)}) collective-permute-start(bf16[2,128,256]{2,1,0:T(8,128)(2,1)S(1)} %collective-permute-done.9.refs_6_.refs_7_), channel_id=1, source_target_pairs={{0,14},{1,3},{2,0},{3,5},{4,2},{5,7},{6,4},{7,9},{8,6},{9,11},{10,... | collective-permute-start | bytes 393224 | tf_op jit(solution)/shard_map/ppermute | solution.py:54
  34.0 1.6 %collective-permute-done.1.refs_0_ = bf16[128,1408]{1,0:T(8,128)(2,1)S(1)} collective-permute-done((bf16[128,1408]{1,0:T(8,128)(2,1)S(1)}, bf16[128,1408]{1,0:T(8,128)(2,1)S(1)}, u32[]{:S(2)}, u32[]{:S(2)}) %collective-permute-start.1) | collective-permute-done | bytes 360480 | tf_op jit(solution)/shard_map/ppermute | solution.py:54
  35.7 2.7 %collective-permute-start.19 = (bf16[2,128,256]{2,1,0:T(8,128)(2,1)S(1)}, bf16[2,128,256]{2,1,0:T(8,128)(2,1)S(1)}, u32[]{:S(2)}, u32[]{:S(2)}) collective-permute-start(bf16[2,128,256]{2,1,0:T(8,128)(2,1)S(1)} %collective-permute-done.18.refs_12_.refs_13_), channel_id=1, source_target_pairs={{0,2},{1,15},{2,4},{3,1},{4,6},{5,3},{6,8},{7,5},{8,10},{9,7},{10,... | collective-permute-start | bytes 393224 | tf_op jit(solution)/shard_map/ppermute | solution.py:54
  38.4 3.8 %collective-permute-done.2.refs_0_ = bf16[128,1408]{1,0:T(8,128)(2,1)S(1)} collective-permute-done((bf16[128,1408]{1,0:T(8,128)(2,1)}, bf16[128,1408]{1,0:T(8,128)(2,1)S(1)}, u32[]{:S(2)}, u32[]{:S(2)}) %collective-permute-start.2) | collective-permute-done | bytes 360480 | tf_op jit(solution)/shard_map/ppermute | solution.py:54
  42.3 1.2 %collective-permute-done.15.refs_9_.refs_10_ = bf16[2,128,256]{2,1,0:T(8,128)(2,1)S(1)} collective-permute-done((bf16[2,128,256]{2,1,0:T(8,128)(2,1)S(1)}, bf16[2,128,256]{2,1,0:T(8,128)(2,1)S(1)}, u32[]{:S(2)}, u32[]{:S(2)}) %collective-permute-start.15) | collective-permute-done | bytes 131104 | tf_op jit(solution)/shard_map/ppermute | solution.py:54
  43.5 0.6 fusion.13
  44.1 9.0 %shard_map.75 = bf16[144,1024]{1,0:T(8,128)(2,1)} custom-call(s32[1,16]{1,0:T(1,128)S(1)} %get-tuple-element.73.slot_ref, s32[1]{0:T(128)} %bitcast.10.length_ref, bf16[128,1408]{1,0:T(8,128)(2,1)S(1)} %collective-permute-done.1.refs_0_, bf16[2,128,256]{2,1,0:T(8,128)(2,1)S(1)} %pad_maximum_fusion.refs_1_.refs_2_, ...), custom_call_target="tpu_custom_call" | custom-call | flops 1 | bytes 1 | tf_op jit(solution)/shard_map/pallas_call | solution.py:202
  53.1 0.8 collective-permute-start.22
  53.9 9.0 %shard_map.76 = bf16[128,1024]{1,0:T(8,128)(2,1)} custom-call(s32[1,16]{1,0:T(1,128)S(1)} %get-tuple-element.74.slot_ref, s32[1]{0:T(128)} %bitcast.9.length_ref, bf16[128,1408]{1,0:T(8,128)(2,1)S(1)} %collective-permute-done.2.refs_0_, bf16[2,128,256]{2,1,0:T(8,128)(2,1)S(1)} %pad_maximum_fusion.refs_1_.refs_2_, ...), custom_call_target="tpu_custom_call" | custom-call | flops 1 | bytes 1 | tf_op jit(solution)/shard_map/pallas_call | solution.py:202
  62.9 5.5 %collective-permute-start.23 = (bf16[128,1024]{1,0:T(8,128)(2,1)}, bf16[128,1024]{1,0:T(8,128)(2,1)S(1)}, u32[]{:S(2)}, u32[]{:S(2)}) collective-permute-start(bf16[128,1024]{1,0:T(8,128)(2,1)} %shard_map.76), channel_id=1, source_target_pairs={{0,17},{1,16},{2,19},{3,18},{4,21},{5,20},{6,23},{7,22},{8,25},{9,... | collective-permute-start | bytes 786440 | tf_op jit(solution)/shard_map/ppermute | solution.py:54
  68.7 11.3 %shard_map.77 = (bf16[64,1024]{1,0:T(8,128)(2,1)S(1)}, bf16[64,1024]{1,0:T(8,128)(2,1)S(1)}, bf16[128,1024]{1,0:T(8,128)(2,1)S(1)}) custom-call(s32[2,16]{1,0:T(2,128)S(1)} %rev.6.slot_ref, s32[2]{0:T(128)S(1)} %rev.7.length_ref, bf16[128,1408]{1,0:T(8,128)(2,1)S(1)} %collective-permute-done.refs_0_, bf16[128,1408]{1,0:T(8,128)(2,1)S(1)} %get-tuple-element.46.refs_1_, ...), custom_call_target="tpu_custom_call" | custom-call | flops 1 | bytes 1 | tf_op jit(solution)/shard_map/pallas_call | solution.py:202
  80.1 0.5 collective-permute-start.21
  80.6 0.8 %collective-permute-done.20.refs_1_ = bf16[64,1024]{1,0:T(8,128)(2,1)S(1)} collective-permute-done((bf16[64,1024]{1,0:T(8,128)(2,1)S(1)}, bf16[64,1024]{1,0:T(8,128)(2,1)S(1)}, u32[]{:S(2)}, u32[]{:S(2)}) %collective-permute-start.20) | collective-permute-done | bytes 131104 | tf_op jit(solution)/shard_map/ppermute | solution.py:54
  81.6 1.5 %shard_map.78 = bf16[128,4096]{1,0:T(8,128)(2,1)} custom-call(s32[4]{0:T(128)S(1)} %pad_add_fusion.head_ref, bf16[128,1024]{1,0:T(8,128)(2,1)S(1)} %get-tuple-element.68.refs_0_, bf16[64,1024]{1,0:T(8,128)(2,1)S(1)} %collective-permute-done.20.refs_1_, bf16[64,1024]{1,0:T(8,128)(2,1)S(1)} %collective-permute-done.21.refs_2_, ...), custom_call_target="tpu_custom_call" | custom-call | tf_op jit(solution)/shard_map/pallas_call | solution.py:268
  (52 shorter events, 1.2 us)
Async XLA Ops:
  0.1 0.9 %copy-start.3 = (bf16[128,512]{1,0:T(8,128)(2,1)S(1)}, bf16[128,512]{1,0:T(8,128)(2,1)}, u32[]{:S(2)}) copy-start(bf16[128,512]{1,0:T(8,128)(2,1)} %k_ref.3) | copy-start | bytes 393220
  1.0 0.9 %copy-start.4 = (bf16[128,512]{1,0:T(8,128)(2,1)S(1)}, bf16[128,512]{1,0:T(8,128)(2,1)}, u32[]{:S(2)}) copy-start(bf16[128,512]{1,0:T(8,128)(2,1)} %v_ref.3) | copy-start | bytes 393220
  2.5 5.0 %collective-permute-start.4 = (bf16[128,256]{1,0:T(8,128)(2,1)S(1)}, bf16[128,256]{1,0:T(8,128)(2,1)S(1)}, u32[]{:S(2)}, u32[]{:S(2)}) collective-permute-start(bf16[128,256]{1,0:T(8,128)(2,1)S(1)} %get-tuple-element.44), channel_id=1, source_target_pairs={{0,16},{1,17},{2,18},{3,19},{4,20},{5,21},{6,22},{7,23},{8,24},{9,... | collective-permute-start | bytes 196616 | tf_op jit(solution)/shard_map/ppermute | solution.py:54
  4.6 5.7 %collective-permute-start.5 = (bf16[128,256]{1,0:T(8,128)(2,1)S(1)}, bf16[128,256]{1,0:T(8,128)(2,1)S(1)}, u32[]{:S(2)}, u32[]{:S(2)}) collective-permute-start(bf16[128,256]{1,0:T(8,128)(2,1)S(1)} %get-tuple-element.45), channel_id=1, source_target_pairs={{0,17},{1,16},{2,19},{3,18},{4,21},{5,20},{6,23},{7,22},{8,25},{9,... | collective-permute-start | bytes 196616 | tf_op jit(solution)/shard_map/ppermute | solution.py:54
  7.4 7.4 %collective-permute-start.3 = (bf16[128,256]{1,0:T(8,128)(2,1)S(1)}, bf16[128,256]{1,0:T(8,128)(2,1)S(1)}, u32[]{:S(2)}, u32[]{:S(2)}) collective-permute-start(bf16[128,256]{1,0:T(8,128)(2,1)S(1)} %get-tuple-element.43), channel_id=1, source_target_pairs={{0,1},{1,0},{2,3},{3,2},{4,5},{5,4},{6,7},{7,6},{8,9},{9,8},{10,11... | collective-permute-start | bytes 196616 | tf_op jit(solution)/shard_map/ppermute | solution.py:54
  10.3 7.3 %copy-start.5 = (s32[1,16]{1,0:T(1,128)S(1)}, s32[1,16]{1,0:T(1,128)}, u32[]{:S(2)}) copy-start(s32[1,16]{1,0:T(1,128)} %param.12) | copy-start | bytes 196
  10.3 8.0 %collective-permute-start.16 = (bf16[2,128,256]{2,1,0:T(8,128)(2,1)S(1)}, bf16[2,128,256]{2,1,0:T(8,128)(2,1)S(1)}, u32[]{:S(2)}, u32[]{:S(2)}) collective-permute-start(bf16[2,128,256]{2,1,0:T(8,128)(2,1)S(1)} %pad_maximum_fusion.1.refs_2_.refs_3_), channel_id=1, source_target_pairs={{0,2},{1,15},{2,4},{3,1},{4,6},{5,3},{6,8},{7,5},{8,10},{9,7},{10,... | collective-permute-start | bytes 393224 | tf_op jit(solution)/shard_map/ppermute | solution.py:54
  14.8 10.7 %collective-permute-start.7 = (bf16[2,128,256]{2,1,0:T(8,128)(2,1)S(1)}, bf16[2,128,256]{2,1,0:T(8,128)(2,1)S(1)}, u32[]{:S(2)}, u32[]{:S(2)}) collective-permute-start(bf16[2,128,256]{2,1,0:T(8,128)(2,1)S(1)} %pad_maximum_fusion.1.refs_2_.refs_3_), channel_id=1, source_target_pairs={{0,14},{1,3},{2,0},{3,5},{4,2},{5,7},{6,4},{7,9},{8,6},{9,11},{10,... | collective-permute-start | bytes 393224 | tf_op jit(solution)/shard_map/ppermute | solution.py:54
  14.8 6.3 %copy-start.1 = (bf16[128,512]{1,0:T(8,128)(2,1)S(1)}, bf16[128,512]{1,0:T(8,128)(2,1)}, u32[]{:S(2)}) copy-start(bf16[128,512]{1,0:T(8,128)(2,1)} %k_ref.2) | copy-start | bytes 393220
  14.8 6.3 %copy-start.2 = (bf16[128,512]{1,0:T(8,128)(2,1)S(1)}, bf16[128,512]{1,0:T(8,128)(2,1)}, u32[]{:S(2)}) copy-start(bf16[128,512]{1,0:T(8,128)(2,1)} %v_ref.2) | copy-start | bytes 393220
  14.9 8.9 %collective-permute-start.12 = (bf16[2,128,256]{2,1,0:T(8,128)(2,1)S(1)}, bf16[2,128,256]{2,1,0:T(8,128)(2,1)S(1)}, u32[]{:S(2)}, u32[]{:S(2)}) collective-permute-start(bf16[2,128,256]{2,1,0:T(8,128)(2,1)S(1)} %pad_maximum_fusion.refs_1_.refs_2_), channel_id=1, source_target_pairs={{0,2},{1,15},{2,4},{3,1},{4,6},{5,3},{6,8},{7,5},{8,10},{9,7},{10,... | collective-permute-start | bytes 393224 | tf_op jit(solution)/shard_map/ppermute | solution.py:54
  18.3 7.8 %collective-permute-start.6 = (bf16[2,128,256]{2,1,0:T(8,128)(2,1)S(1)}, bf16[2,128,256]{2,1,0:T(8,128)(2,1)S(1)}, u32[]{:S(2)}, u32[]{:S(2)}) collective-permute-start(bf16[2,128,256]{2,1,0:T(8,128)(2,1)S(1)} %pad_maximum_fusion.refs_1_.refs_2_), channel_id=1, source_target_pairs={{0,14},{1,3},{2,0},{3,5},{4,2},{5,7},{6,4},{7,9},{8,6},{9,11},{10,... | collective-permute-start | bytes 393224 | tf_op jit(solution)/shard_map/ppermute | solution.py:54
  18.4 8.0 %collective-permute-start.17 = (bf16[2,128,256]{2,1,0:T(8,128)(2,1)S(1)}, bf16[2,128,256]{2,1,0:T(8,128)(2,1)S(1)}, u32[]{:S(2)}, u32[]{:S(2)}) collective-permute-start(bf16[2,128,256]{2,1,0:T(8,128)(2,1)S(1)} %collective-permute-done.16.refs_16_.refs_17_), channel_id=1, source_target_pairs={{0,2},{1,15},{2,4},{3,1},{4,6},{5,3},{6,8},{7,5},{8,10},{9,7},{10,... | collective-permute-start | bytes 393224 | tf_op jit(solution)/shard_map/ppermute | solution.py:54
  21.1 1.2 %copy-start = (bf16[128,4096]{1,0:T(8,128)(2,1)S(1)}, bf16[128,4096]{1,0:T(8,128)(2,1)}, u32[]{:S(2)}) copy-start(bf16[128,4096]{1,0:T(8,128)(2,1)} %q_ref.1) | copy-start | bytes 3145732
  23.8 9.2 %collective-permute-start = (bf16[128,1408]{1,0:T(8,128)(2,1)S(1)}, bf16[128,1408]{1,0:T(8,128)(2,1)S(1)}, u32[]{:S(2)}, u32[]{:S(2)}) collective-permute-start(bf16[128,1408]{1,0:T(8,128)(2,1)S(1)} %get-tuple-element.39), channel_id=1, source_target_pairs={{0,1},{1,0},{2,3},{3,2},{4,5},{5,4},{6,7},{7,6},{8,9},{9,8},{10,11... | collective-permute-start | bytes 1081352 | tf_op jit(solution)/shard_map/ppermute | solution.py:54
  23.8 4.1 %collective-permute-start.13 = (bf16[2,128,256]{2,1,0:T(8,128)(2,1)S(1)}, bf16[2,128,256]{2,1,0:T(8,128)(2,1)S(1)}, u32[]{:S(2)}, u32[]{:S(2)}) collective-permute-start(bf16[2,128,256]{2,1,0:T(8,128)(2,1)S(1)} %collective-permute-done.12.refs_15_.refs_16_), channel_id=1, source_target_pairs={{0,2},{1,15},{2,4},{3,1},{4,6},{5,3},{6,8},{7,5},{8,10},{9,7},{10,... | collective-permute-start | bytes 393224 | tf_op jit(solution)/shard_map/ppermute | solution.py:54
  25.6 10.1 %collective-permute-start.1 = (bf16[128,1408]{1,0:T(8,128)(2,1)S(1)}, bf16[128,1408]{1,0:T(8,128)(2,1)S(1)}, u32[]{:S(2)}, u32[]{:S(2)}) collective-permute-start(bf16[128,1408]{1,0:T(8,128)(2,1)S(1)} %get-tuple-element.40), channel_id=1, source_target_pairs={{0,16},{1,17},{2,18},{3,19},{4,20},{5,21},{6,22},{7,23},{8,24},{9,... | collective-permute-start | bytes 1081352 | tf_op jit(solution)/shard_map/ppermute | solution.py:54
  26.1 5.7 %collective-permute-start.9 = (bf16[2,128,256]{2,1,0:T(8,128)(2,1)S(1)}, bf16[2,128,256]{2,1,0:T(8,128)(2,1)S(1)}, u32[]{:S(2)}, u32[]{:S(2)}) collective-permute-start(bf16[2,128,256]{2,1,0:T(8,128)(2,1)S(1)} %collective-permute-done.7.refs_4_.refs_5_), channel_id=1, source_target_pairs={{0,14},{1,3},{2,0},{3,5},{4,2},{5,7},{6,4},{7,9},{8,6},{9,11},{10,... | collective-permute-start | bytes 393224 | tf_op jit(solution)/shard_map/ppermute | solution.py:54
  26.4 6.2 %collective-permute-start.8 = (bf16[2,128,256]{2,1,0:T(8,128)(2,1)S(1)}, bf16[2,128,256]{2,1,0:T(8,128)(2,1)S(1)}, u32[]{:S(2)}, u32[]{:S(2)}) collective-permute-start(bf16[2,128,256]{2,1,0:T(8,128)(2,1)S(1)} %collective-permute-done.6.refs_3_.refs_4_), channel_id=1, source_target_pairs={{0,14},{1,3},{2,0},{3,5},{4,2},{5,7},{6,4},{7,9},{8,6},{9,11},{10,... | collective-permute-start | bytes 393224 | tf_op jit(solution)/shard_map/ppermute | solution.py:54
  27.9 14.4 %collective-permute-start.2 = (bf16[128,1408]{1,0:T(8,128)(2,1)}, bf16[128,1408]{1,0:T(8,128)(2,1)S(1)}, u32[]{:S(2)}, u32[]{:S(2)}) collective-permute-start(bf16[128,1408]{1,0:T(8,128)(2,1)} %get-tuple-element.41), channel_id=1, source_target_pairs={{0,17},{1,16},{2,19},{3,18},{4,21},{5,20},{6,23},{7,22},{8,25},{9,... | collective-permute-start | bytes 1081352 | tf_op jit(solution)/shard_map/ppermute | solution.py:54
  31.7 4.0 %collective-permute-start.18 = (bf16[2,128,256]{2,1,0:T(8,128)(2,1)S(1)}, bf16[2,128,256]{2,1,0:T(8,128)(2,1)S(1)}, u32[]{:S(2)}, u32[]{:S(2)}) collective-permute-start(bf16[2,128,256]{2,1,0:T(8,128)(2,1)S(1)} %collective-permute-done.17.refs_14_.refs_15_), channel_id=1, source_target_pairs={{0,2},{1,15},{2,4},{3,1},{4,6},{5,3},{6,8},{7,5},{8,10},{9,7},{10,... | collective-permute-start | bytes 393224 | tf_op jit(solution)/shard_map/ppermute | solution.py:54
  32.6 5.8 %collective-permute-start.14 = (bf16[2,128,256]{2,1,0:T(8,128)(2,1)S(1)}, bf16[2,128,256]{2,1,0:T(8,128)(2,1)S(1)}, u32[]{:S(2)}, u32[]{:S(2)}) collective-permute-start(bf16[2,128,256]{2,1,0:T(8,128)(2,1)S(1)} %collective-permute-done.13.refs_13_.refs_14_), channel_id=1, source_target_pairs={{0,2},{1,15},{2,4},{3,1},{4,6},{5,3},{6,8},{7,5},{8,10},{9,7},{10,... | collective-permute-start | bytes 393224 | tf_op jit(solution)/shard_map/ppermute | solution.py:54
  33.0 9.3 %collective-permute-start.11 = (bf16[2,128,256]{2,1,0:T(8,128)(2,1)S(1)}, bf16[2,128,256]{2,1,0:T(8,128)(2,1)S(1)}, u32[]{:S(2)}, u32[]{:S(2)}) collective-permute-start(bf16[2,128,256]{2,1,0:T(8,128)(2,1)S(1)} %collective-permute-done.9.refs_6_.refs_7_), channel_id=1, source_target_pairs={{0,14},{1,3},{2,0},{3,5},{4,2},{5,7},{6,4},{7,9},{8,6},{9,11},{10,... | collective-permute-start | bytes 393224 | tf_op jit(solution)/shard_map/ppermute | solution.py:54
  35.7 6.6 %collective-permute-start.10 = (bf16[2,128,256]{2,1,0:T(8,128)(2,1)S(1)}, bf16[2,128,256]{2,1,0:T(8,128)(2,1)S(1)}, u32[]{:S(2)}, u32[]{:S(2)}) collective-permute-start(bf16[2,128,256]{2,1,0:T(8,128)(2,1)S(1)} %collective-permute-done.8.refs_5_.refs_6_), channel_id=1, source_target_pairs={{0,14},{1,3},{2,0},{3,5},{4,2},{5,7},{6,4},{7,9},{8,6},{9,11},{10,... | collective-permute-start | bytes 393224 | tf_op jit(solution)/shard_map/ppermute | solution.py:54
  35.7 6.6 %collective-permute-start.19 = (bf16[2,128,256]{2,1,0:T(8,128)(2,1)S(1)}, bf16[2,128,256]{2,1,0:T(8,128)(2,1)S(1)}, u32[]{:S(2)}, u32[]{:S(2)}) collective-permute-start(bf16[2,128,256]{2,1,0:T(8,128)(2,1)S(1)} %collective-permute-done.18.refs_12_.refs_13_), channel_id=1, source_target_pairs={{0,2},{1,15},{2,4},{3,1},{4,6},{5,3},{6,8},{7,5},{8,10},{9,7},{10,... | collective-permute-start | bytes 393224 | tf_op jit(solution)/shard_map/ppermute | solution.py:54
  38.4 5.1 %collective-permute-start.15 = (bf16[2,128,256]{2,1,0:T(8,128)(2,1)S(1)}, bf16[2,128,256]{2,1,0:T(8,128)(2,1)S(1)}, u32[]{:S(2)}, u32[]{:S(2)}) collective-permute-start(bf16[2,128,256]{2,1,0:T(8,128)(2,1)S(1)} %collective-permute-done.14.refs_11_.refs_12_), channel_id=1, source_target_pairs={{0,2},{1,15},{2,4},{3,1},{4,6},{5,3},{6,8},{7,5},{8,10},{9,7},{10,... | collective-permute-start | bytes 393224 | tf_op jit(solution)/shard_map/ppermute | solution.py:54
  53.1 28.5 %collective-permute-start.22 = (bf16[144,1024]{1,0:T(8,128)(2,1)}, bf16[144,1024]{1,0:T(8,128)(2,1)S(1)}, u32[]{:S(2)}, u32[]{:S(2)}) collective-permute-start(bf16[144,1024]{1,0:T(8,128)(2,1)} %shard_map.75), channel_id=1, source_target_pairs={{0,16},{1,17},{2,18},{3,19},{4,20},{5,21},{6,22},{7,23},{8,24},{9,... | collective-permute-start | bytes 884744 | tf_op jit(solution)/shard_map/ppermute | solution.py:54
  62.9 18.7 %collective-permute-start.23 = (bf16[128,1024]{1,0:T(8,128)(2,1)}, bf16[128,1024]{1,0:T(8,128)(2,1)S(1)}, u32[]{:S(2)}, u32[]{:S(2)}) collective-permute-start(bf16[128,1024]{1,0:T(8,128)(2,1)} %shard_map.76), channel_id=1, source_target_pairs={{0,17},{1,16},{2,19},{3,18},{4,21},{5,20},{6,23},{7,22},{8,25},{9,... | collective-permute-start | bytes 786440 | tf_op jit(solution)/shard_map/ppermute | solution.py:54
  80.0 1.4 %collective-permute-start.20 = (bf16[64,1024]{1,0:T(8,128)(2,1)S(1)}, bf16[64,1024]{1,0:T(8,128)(2,1)S(1)}, u32[]{:S(2)}, u32[]{:S(2)}) collective-permute-start(bf16[64,1024]{1,0:T(8,128)(2,1)S(1)} %get-tuple-element.69), channel_id=1, source_target_pairs={{0,1},{1,0},{2,3},{3,2},{4,5},{5,4},{6,7},{7,6},{8,9},{9,8},{10,11... | collective-permute-start | bytes 393224 | tf_op jit(solution)/shard_map/ppermute | solution.py:54
  80.1 1.5 %collective-permute-start.21 = (bf16[64,1024]{1,0:T(8,128)(2,1)S(1)}, bf16[64,1024]{1,0:T(8,128)(2,1)S(1)}, u32[]{:S(2)}, u32[]{:S(2)}) collective-permute-start(bf16[64,1024]{1,0:T(8,128)(2,1)S(1)} %get-tuple-element.70), channel_id=1, source_target_pairs={{0,1},{1,0},{2,3},{3,2},{4,5},{5,4},{6,7},{7,6},{8,9},{9,8},{10,11... | collective-permute-start | bytes 393224 | tf_op jit(solution)/shard_map/ppermute | solution.py:54
